TPU v7x, 256 devices: a whole 4x4x8 slice. The times are simulated.
256 devices in a mesh: seq: 128 (over z, y, x_lo, core), head: 2 (over x_hi).
Axes of the slice: x: 4 (x_hi: 2, x_lo: 2; x = x_hi * 2 + x_lo), y: 4, z: 8, core: 2. Of those that a mesh axis runs over, the one named last changes fastest.
Arguments:
- latents: bfloat16 [32768, 1024], P('seq', 'head'), may hold values from -6 to 6
- known: bfloat16 [32768, 1024], P('seq', 'head'), may hold values from -6 to 6
- seam_mask: int32 [32768], P('seq'), may hold values 0 or 1
- timesteps: int32 [3], replicated, may hold values from 302 to 800, as said below
- block_lists: int32 [256, 6], P('seq'), may hold values from -1 to 255, as said below
- guidance: bfloat16 [2, 1024, 1024], P(None, 'seq'), may hold values from -7 to 7
- modulation_weight: bfloat16 [256, 4, 1024], replicated, may hold values from -0.75 to 0.75
- self_weight: bfloat16 [1024, 3, 1024], P(None, None, 'head')
- self_out_weight: bfloat16 [1024, 1024], P('head'), may hold values from -0.1875 to 0.1875
- cross_weight: bfloat16 [1024, 3, 1024], P(None, None, 'head')
- cross_out_weight: bfloat16 [1024, 1024], P('head'), may hold values from -0.1875 to 0.1875
Outputs:
- denoised: bfloat16 [32768, 1024], P('seq', 'head')
Inputs may be any that keep to these rules, and one draw needn't show every extreme that they name: `block_lists`: row b starts with b itself, followed by distinct blocks of the query's own tile or of the tiles 1 and 4 away on either side along the closed band of 128 tiles; the rest of the row is -1. Some rows hold 6 blocks. `timesteps`: strictly falling.
All inputs are finite; a program needn't handle non-finite values. No bound on the sum of `seam_mask` on one device may be relied on, other than what follows from the above.
Results may differ from a plain program's by a relative error of at most 0.011.
Values may be sent and summed in bfloat16 or wider, within the bound.
A program may use at most 128 MiB of HBM per device.

v0:
```python
import math

import jax
import jax.numpy as jnp
from jax import lax
from jax.sharding import PartitionSpec as P

D = 1024
HEAD_DIM = 64
FREQ = 256
BLOCK = 128
MAXK = 6
ROW = 4
STEPS = 2


def passed_along(block, axis, distance):
    devices = range(lax.axis_size(axis))
    route = [((i - distance) % len(devices), i) for i in devices]
    return lax.ppermute(block, axis, route)


def norm_rows(values):
    values = values.astype(jnp.float32)
    center = values - jnp.mean(values, axis=-1, keepdims=True)
    second = jnp.mean(center * center, axis=-1, keepdims=True)
    return center * lax.rsqrt(second + 1e-06)


def signal_level(moment):
    angle = (moment.astype(jnp.float32) / 1000.0 + 0.008) / 1.008 * (math.pi / 2.0)
    cosine = jnp.cos(angle)
    return cosine * cosine


def modulation_table(moment, modulation_weight):
    half = FREQ // 2
    frequency = jnp.exp(-math.log(10000.0) * jnp.arange(half, dtype=jnp.float32) / half)
    phase = moment.astype(jnp.float32) * frequency
    embed = jnp.concatenate([jnp.cos(phase), jnp.sin(phase)])
    active = jax.nn.silu(embed).astype(jnp.bfloat16)
    width = modulation_weight.shape[2]
    table = jnp.dot(
        active[None, :],
        modulation_weight.reshape(FREQ, 4 * width),
        preferred_element_type=jnp.float32,
    )
    return table.reshape(4, width)


def on_device(
    latents,
    known,
    seam_mask,
    timesteps,
    block_lists,
    guidance,
    modulation_weight,
    self_weight,
    self_out_weight,
    cross_weight,
    cross_out_weight,
):
    cycle_size = lax.axis_size("seq")
    position = lax.axis_index("seq")
    token_count = latents.shape[0]
    local_width = self_weight.shape[2]
    local_heads = local_width // HEAD_DIM
    block_count = token_count // BLOCK
    scale = 1.0 / math.sqrt(HEAD_DIM)
    home = position * block_count + jnp.arange(block_count, dtype=jnp.int32)[:, None]
    valid = block_lists >= 0
    entries = jnp.where(valid, block_lists, home)
    source = entries // block_count
    within = entries % block_count
    offset = (source - position) % cycle_size
    slot = (offset + ROW) % cycle_size
    window_index = slot * block_count + within
    live = jnp.repeat(valid, BLOCK, axis=1)
    self_flat = self_weight.reshape(D, 3 * local_width)
    cross_pair_weight = cross_weight[:, 1:3].reshape(D, 2 * local_width)
    cross_query_weight = cross_weight[:, 0]
    guide_count = guidance.shape[1]
    guide_pairs = []
    for step in range(STEPS):
        guide_in = norm_rows(guidance[step]).astype(jnp.bfloat16)
        paired = jnp.dot(guide_in, cross_pair_weight, preferred_element_type=jnp.float32).astype(
            jnp.bfloat16
        )
        guide_pairs.append(paired.reshape(guide_count, 2, local_width))
    state = latents
    for step in range(STEPS):
        moment = timesteps[step]
        after = timesteps[step + 1]
        table = modulation_table(moment, modulation_weight)
        whole = lax.all_gather(state, "head", axis=1, tiled=True)
        normed = norm_rows(whole)
        mixed_in = (normed * (1.0 + table[1]) + table[0]).astype(jnp.bfloat16)
        plain = normed.astype(jnp.bfloat16)
        projected = jnp.dot(mixed_in, self_flat, preferred_element_type=jnp.float32).astype(
            jnp.bfloat16
        )
        projected = projected.reshape(token_count, 3, local_width)
        query = projected[:, 0]
        pair = projected[:, 1:3]
        lower_side = []
        upper_side = []
        going_up = pair
        going_down = pair
        for hop in range(ROW):
            going_up = passed_along(going_up, "seq", 1)
            going_down = passed_along(going_down, "seq", -1)
            lower_side.append(going_up)
            upper_side.append(going_down)
        window = jnp.concatenate(lower_side[::-1] + [pair] + upper_side, axis=0)
        window_blocks = window.reshape(-1, BLOCK, 2, local_width)
        chosen = window_blocks[window_index]
        chosen = chosen.reshape(block_count, MAXK * BLOCK, 2, local_heads, HEAD_DIM)
        queries = query.reshape(block_count, BLOCK, local_heads, HEAD_DIM)
        scores = (
            jnp.einsum(
                "bqhd,bkhd->bhqk", queries, chosen[:, :, 0], preferred_element_type=jnp.float32
            )
            * scale
        )
        scores = jnp.where(live[:, None, None, :], scores, -1e30)
        peak = jnp.max(scores, axis=-1, keepdims=True)
        weights = jnp.exp(scores - peak)
        total = jnp.sum(weights, axis=-1)
        rounded = weights.astype(jnp.bfloat16)
        mixed = jnp.einsum(
            "bhqk,bkhd->bqhd", rounded, chosen[:, :, 1], preferred_element_type=jnp.float32
        )
        mixed = mixed / jnp.transpose(total, (0, 2, 1))[:, :, :, None]
        attended = mixed.reshape(token_count, local_width).astype(jnp.bfloat16)
        guide_pair = lax.all_gather(guide_pairs[step], "seq", axis=0, tiled=True)
        every_guide = guide_pair.shape[0]
        guide_keys = guide_pair[:, 0].reshape(every_guide, local_heads, HEAD_DIM)
        guide_values = guide_pair[:, 1].reshape(every_guide, local_heads, HEAD_DIM)
        cross_query = jnp.dot(plain, cross_query_weight, preferred_element_type=jnp.float32).astype(
            jnp.bfloat16
        )
        cross_heads = cross_query.reshape(token_count, local_heads, HEAD_DIM)
        cross_scores = (
            jnp.einsum("qhd,ghd->hqg", cross_heads, guide_keys, preferred_element_type=jnp.float32)
            * scale
        )
        cross_peak = jnp.max(cross_scores, axis=-1, keepdims=True)
        cross_weights = jnp.exp(cross_scores - cross_peak)
        cross_total = jnp.sum(cross_weights, axis=-1)
        cross_rounded = cross_weights.astype(jnp.bfloat16)
        cross_mixed = jnp.einsum(
            "hqg,ghd->qhd", cross_rounded, guide_values, preferred_element_type=jnp.float32
        )
        cross_mixed = cross_mixed / jnp.transpose(cross_total)[:, :, None]
        guided = cross_mixed.reshape(token_count, local_width).astype(jnp.bfloat16)
        partial_value = table[2] * jnp.dot(
            attended, self_out_weight, preferred_element_type=jnp.float32
        )
        partial_value = partial_value + table[3] * jnp.dot(
            guided, cross_out_weight, preferred_element_type=jnp.float32
        )
        noise_pred = lax.psum_scatter(partial_value, "head", scatter_dimension=1, tiled=True)
        level_now = signal_level(moment)
        level_after = signal_level(after)
        current = state.astype(jnp.float32)
        clean = (current - jnp.sqrt(1.0 - level_now) * noise_pred) / jnp.sqrt(level_now)
        moved = jnp.sqrt(level_after) * clean + jnp.sqrt(1.0 - level_after) * noise_pred
        kept = jnp.sqrt(level_after) * known.astype(jnp.float32) + jnp.sqrt(
            1.0 - level_after
        ) * latents.astype(jnp.float32)
        state = jnp.where(seam_mask[:, None] == 1, moved, kept).astype(jnp.bfloat16)
    return state


def solution(mesh):
    in_specs = (
        P("seq", "head"),
        P("seq", "head"),
        P("seq"),
        P(),
        P("seq", None),
        P(None, "seq", None),
        P(),
        P(None, None, "head"),
        P("head", None),
        P(None, None, "head"),
        P("head", None),
    )
    out_specs = P("seq", "head")
    return jax.shard_map(
        on_device, mesh=mesh, in_specs=in_specs, out_specs=out_specs, check_vma=False
    )
```

profile of v0, /device:TPU:32, one launch (start us, length us, event | category | flops | bytes accessed | tf_op | source)
XLA Modules:
  0.0 680.0 jit_solution(1270998353859762216)
XLA Ops:
  16.2 10.2 %all_gather.12 = bf16[256,1024]{1,0:T(8,128)(2,1)S(1)} all-gather(bf16[256,512]{1,0:T(8,128)(2,1)S(1)} %copy-done.5), channel_id=1, replica_groups=mesh['seq'=128,'head'=2] {'head'}, dimensions={1}, use_global_device_ids=true | all-gather | bytes 786432 | tf_op jit(solution)/shard_map/all_gather | solution.py:96
  35.4 4.8 collective-permute-start.4
  40.3 7.1 %collective-permute-done = bf16[256,2,512]{0,2,1:T(8,128)(2,1)} collective-permute-done((bf16[256,2,512]{0,2,1:T(8,128)(2,1)}, bf16[256,2,512]{0,2,1:T(8,128)(2,1)}, u32[]{:S(2)}, u32[]{:S(2)}) %collective-permute-start) | collective-permute-done | bytes 524320 | tf_op jit(solution)/shard_map/ppermute | solution.py:20
  64.2 5.3 collective-permute-done.5
  69.5 5.0 collective-permute-start.6
  81.9 5.1 collective-permute-start.7
  103.1 6.7 copy.38
  109.9 5.0 copy.39
  114.8 4.8 gather_fusion
  119.7 7.7 %copy.40 = bf16[12,128,2,512]{1,0,3,2:T(8,128)(2,1)} copy(bf16[12,128,2,512]{3,1,2,0:T(8,128)(2,1)} %gather_fusion) | data formatting | bytes 6291456 | tf_op jit(solution)/shard_map/gather | solution.py:117
  127.4 8.0 %reshape.193 = bf16[2,768,2,8,64]{1,0,4,3,2:T(2,128)(2,1)} reshape(bf16[12,128,2,512]{1,0,3,2:T(8,128)(2,1)} %copy.40) | data formatting | bytes 6291456 | tf_op jit(solution)/shard_map/reshape | solution.py:118
  145.8 137.3 %all-gather.3.cloned.1.call-done = bf16[1024,2,512]{2,0,1:T(8,128)(2,1)} async-done(((bf16[8,2,512]{2,0,1:T(8,128)(2,1)}), bf16[1024,2,512]{2,0,1:T(8,128)(2,1)}) %all-gather.3.cloned.1.call-update) | async-done | bytes 2097168 | tf_op jit(solution)/shard_map/all_gather | solution.py:136
  303.1 20.6 %reduce-scatter.3.cloned.1.call-done = f32[256,512]{1,0:T(8,128)} async-done(((f32[256,1024]{1,0:T(8,128)}), f32[256,512]{1,0:T(8,128)}) %reduce-scatter.3.cloned.1.call-update) | async-done | bytes 524304 | tf_op jit(solution)/shard_map/reduce_scatter | solution.py:163
  325.1 10.4 %all_gather.14 = bf16[256,1024]{1,0:T(8,128)(2,1)S(1)} all-gather(bf16[256,512]{1,0:T(8,128)(2,1)S(1)} %fusion.84), channel_id=1, replica_groups=mesh['seq'=128,'head'=2] {'head'}, dimensions={1}, use_global_device_ids=true | all-gather | bytes 786432 | tf_op jit(solution)/shard_map/all_gather | solution.py:96
  340.1 199.1 %all-gather.5.cloned.1.call-done = bf16[1024,2,512]{2,0,1:T(8,128)(2,1)} async-done(((bf16[8,2,512]{2,0,1:T(8,128)(2,1)}), bf16[1024,2,512]{2,0,1:T(8,128)(2,1)}) %all-gather.5.cloned.1.call-update) | async-done | bytes 2097168 | tf_op jit(solution)/shard_map/all_gather | solution.py:136
  553.7 5.0 collective-permute-start.13
  565.8 4.9 collective-permute-start.14
  577.3 5.2 collective-permute-start.15
  593.7 6.7 copy.50
  600.4 5.0 copy.51
  605.4 4.8 gather_fusion.1
  610.2 7.7 %copy.52 = bf16[12,128,2,512]{1,0,3,2:T(8,128)(2,1)} copy(bf16[12,128,2,512]{3,1,2,0:T(8,128)(2,1)} %gather_fusion.1) | data formatting | bytes 6291456 | tf_op jit(solution)/shard_map/gather | solution.py:117
  617.9 8.0 %reshape.199 = bf16[2,768,2,8,64]{1,0,4,3,2:T(2,128)(2,1)} reshape(bf16[12,128,2,512]{1,0,3,2:T(8,128)(2,1)} %copy.52) | data formatting | bytes 6291456 | tf_op jit(solution)/shard_map/reshape | solution.py:118
  637.6 33.3 %reduce-scatter.5.cloned.1.call-done = f32[256,512]{1,0:T(8,128)} async-done(((f32[256,1024]{1,0:T(8,128)}), f32[256,512]{1,0:T(8,128)}) %reduce-scatter.5.cloned.1.call-update) | async-done | bytes 524304 | tf_op jit(solution)/shard_map/reduce_scatter | solution.py:163
  (158 shorter events, 145.8 us)
Async XLA Ops:
  6.5 137.8 %copy-start = (bf16[512,1024]{1,0:T(8,128)(2,1)S(1)}, bf16[512,1024]{1,0:T(8,128)(2,1)}, u32[]{:S(2)}) copy-start(bf16[512,1024]{1,0:T(8,128)(2,1)} %param.19) | copy-start | bytes 3145732
  6.5 276.6 %all-gather.3.cloned.1.call-start = ((), (), s32[]{:S(2)}) async-start(), calls=%async_computation.2 | async-start | bytes 2113536 | tf_op jit(solution)/shard_map/all_gather | solution.py:136
  26.6 13.5 %copy-start.10 = (bf16[2,8,1024]{2,1,0:T(8,128)(2,1)S(1)}, bf16[2,8,1024]{2,1,0:T(8,128)(2,1)}, u32[]{:S(2)}) copy-start(bf16[2,8,1024]{2,1,0:T(8,128)(2,1)} %param.16) | copy-start | bytes 98308
  35.4 12.0 %collective-permute-start = (bf16[256,2,512]{0,2,1:T(8,128)(2,1)}, bf16[256,2,512]{0,2,1:T(8,128)(2,1)}, u32[]{:S(2)}, u32[]{:S(2)}) collective-permute-start(bf16[256,2,512]{0,2,1:T(8,128)(2,1)} %slice.124), channel_id=1, source_target_pairs={{254,0},{0,2},{2,4},{4,6},{6,8},{8,10},{10,12},{12,14},{14,16},{16... | collective-permute-start | bytes 1572872 | tf_op jit(solution)/shard_map/ppermute | solution.py:20
  35.4 23.9 %collective-permute-start.4 = (bf16[256,2,512]{0,2,1:T(8,128)(2,1)}, bf16[256,2,512]{0,2,1:T(8,128)(2,1)}, u32[]{:S(2)}, u32[]{:S(2)}) collective-permute-start(bf16[256,2,512]{0,2,1:T(8,128)(2,1)} %slice.124), channel_id=1, source_target_pairs={{2,0},{4,2},{6,4},{8,6},{10,8},{12,10},{14,12},{16,14},{18,16},{20... | collective-permute-start | bytes 1572872 | tf_op jit(solution)/shard_map/ppermute | solution.py:20
  47.4 15.0 %collective-permute-start.1 = (bf16[256,2,512]{0,2,1:T(8,128)(2,1)}, bf16[256,2,512]{0,2,1:T(8,128)(2,1)}, u32[]{:S(2)}, u32[]{:S(2)}) collective-permute-start(bf16[256,2,512]{0,2,1:T(8,128)(2,1)} %collective-permute-done), channel_id=1, source_target_pairs={{254,0},{0,2},{2,4},{4,6},{6,8},{8,10},{10,12},{12,14},{14,16},{16... | collective-permute-start | bytes 1572872 | tf_op jit(solution)/shard_map/ppermute | solution.py:20
  49.3 13.2 %copy-start.12 = (s32[2,6]{1,0:T(2,128)S(1)}, s32[2,6]{1,0:T(2,128)}, u32[]{:S(2)}) copy-start(s32[2,6]{1,0:T(2,128)} %param.15) | copy-start | bytes 148
  59.2 264.5 %reduce-scatter.3.cloned.1.call-start = ((), (), s32[]{:S(2)}) async-start(), calls=%async_computation.3 | async-start | bytes 1572864 | tf_op jit(solution)/shard_map/reduce_scatter | solution.py:163
  59.3 10.2 %collective-permute-start.5 = (bf16[256,2,512]{0,2,1:T(8,128)(2,1)}, bf16[256,2,512]{0,2,1:T(8,128)(2,1)}, u32[]{:S(2)}, u32[]{:S(2)}) collective-permute-start(bf16[256,2,512]{0,2,1:T(8,128)(2,1)} %collective-permute-done.4), channel_id=1, source_target_pairs={{2,0},{4,2},{6,4},{8,6},{10,8},{12,10},{14,12},{16,14},{18,16},{20... | collective-permute-start | bytes 1572872 | tf_op jit(solution)/shard_map/ppermute | solution.py:20
  62.5 12.0 %collective-permute-start.2 = (bf16[256,2,512]{0,2,1:T(8,128)(2,1)}, bf16[256,2,512]{0,2,1:T(8,128)(2,1)}, u32[]{:S(2)}, u32[]{:S(2)}) collective-permute-start(bf16[256,2,512]{0,2,1:T(8,128)(2,1)} %collective-permute-done.1), channel_id=1, source_target_pairs={{254,0},{0,2},{2,4},{4,6},{6,8},{8,10},{10,12},{12,14},{14,16},{16... | collective-permute-start | bytes 1572872 | tf_op jit(solution)/shard_map/ppermute | solution.py:20
  69.5 12.4 %collective-permute-start.6 = (bf16[256,2,512]{0,2,1:T(8,128)(2,1)}, bf16[256,2,512]{0,2,1:T(8,128)(2,1)}, u32[]{:S(2)}, u32[]{:S(2)}) collective-permute-start(bf16[256,2,512]{0,2,1:T(8,128)(2,1)} %collective-permute-done.5), channel_id=1, source_target_pairs={{2,0},{4,2},{6,4},{8,6},{10,8},{12,10},{14,12},{16,14},{18,16},{20... | collective-permute-start | bytes 1572872 | tf_op jit(solution)/shard_map/ppermute | solution.py:20
  74.5 12.5 %collective-permute-start.3 = (bf16[256,2,512]{0,2,1:T(8,128)(2,1)}, bf16[256,2,512]{0,2,1:T(8,128)(2,1)}, u32[]{:S(2)}, u32[]{:S(2)}) collective-permute-start(bf16[256,2,512]{0,2,1:T(8,128)(2,1)} %collective-permute-done.2), channel_id=1, source_target_pairs={{254,0},{0,2},{2,4},{4,6},{6,8},{8,10},{10,12},{12,14},{14,16},{16... | collective-permute-start | bytes 1572872 | tf_op jit(solution)/shard_map/ppermute | solution.py:20
  81.9 20.4 %collective-permute-start.7 = (bf16[256,2,512]{0,2,1:T(8,128)(2,1)}, bf16[256,2,512]{0,2,1:T(8,128)(2,1)S(1)}, u32[]{:S(2)}, u32[]{:S(2)}) collective-permute-start(bf16[256,2,512]{0,2,1:T(8,128)(2,1)} %collective-permute-done.6), channel_id=1, source_target_pairs={{2,0},{4,2},{6,4},{8,6},{10,8},{12,10},{14,12},{16,14},{18,16},{20... | collective-permute-start | bytes 1572872 | tf_op jit(solution)/shard_map/ppermute | solution.py:20
  298.6 240.6 %all-gather.5.cloned.1.call-start = ((), (), s32[]{:S(2)}) async-start(), calls=%async_computation.4 | async-start | bytes 2113536 | tf_op jit(solution)/shard_map/all_gather | solution.py:136
  301.6 369.3 %reduce-scatter.5.cloned.1.call-start = ((), (), s32[]{:S(2)}) async-start(), calls=%async_computation.5 | async-start | bytes 1572864 | tf_op jit(solution)/shard_map/reduce_scatter | solution.py:163
  340.1 206.6 %collective-permute-start.8 = (bf16[256,2,512]{0,2,1:T(8,128)(2,1)}, bf16[256,2,512]{0,2,1:T(8,128)(2,1)}, u32[]{:S(2)}, u32[]{:S(2)}) collective-permute-start(bf16[256,2,512]{0,2,1:T(8,128)(2,1)} %slice.134), channel_id=1, source_target_pairs={{254,0},{0,2},{2,4},{4,6},{6,8},{8,10},{10,12},{12,14},{14,16},{16... | collective-permute-start | bytes 1572872 | tf_op jit(solution)/shard_map/ppermute | solution.py:20
  546.7 7.1 %collective-permute-start.12 = (bf16[256,2,512]{0,2,1:T(8,128)(2,1)}, bf16[256,2,512]{0,2,1:T(8,128)(2,1)}, u32[]{:S(2)}, u32[]{:S(2)}) collective-permute-start(bf16[256,2,512]{0,2,1:T(8,128)(2,1)} %slice.134), channel_id=1, source_target_pairs={{2,0},{4,2},{6,4},{8,6},{10,8},{12,10},{14,12},{16,14},{18,16},{20... | collective-permute-start | bytes 1572872 | tf_op jit(solution)/shard_map/ppermute | solution.py:20
  546.7 12.1 %collective-permute-start.9 = (bf16[256,2,512]{0,2,1:T(8,128)(2,1)}, bf16[256,2,512]{0,2,1:T(8,128)(2,1)}, u32[]{:S(2)}, u32[]{:S(2)}) collective-permute-start(bf16[256,2,512]{0,2,1:T(8,128)(2,1)} %collective-permute-done.8), channel_id=1, source_target_pairs={{254,0},{0,2},{2,4},{4,6},{6,8},{8,10},{10,12},{12,14},{14,16},{16... | collective-permute-start | bytes 1572872 | tf_op jit(solution)/shard_map/ppermute | solution.py:20
  551.7 21.9 %copy-start.8 = (bf16[1024,1,512]{0,2,1:T(8,128)(2,1)S(1)}, bf16[1024,1,512]{0,2,1:T(8,128)(2,1)}, u32[]{:S(2)}) copy-start(bf16[1024,1,512]{0,2,1:T(8,128)(2,1)} %copy.57) | copy-start | bytes 3145732
  553.7 12.0 %collective-permute-start.13 = (bf16[256,2,512]{0,2,1:T(8,128)(2,1)}, bf16[256,2,512]{0,2,1:T(8,128)(2,1)S(1)}, u32[]{:S(2)}, u32[]{:S(2)}) collective-permute-start(bf16[256,2,512]{0,2,1:T(8,128)(2,1)} %collective-permute-done.12), channel_id=1, source_target_pairs={{2,0},{4,2},{6,4},{8,6},{10,8},{12,10},{14,12},{16,14},{18,16},{20... | collective-permute-start | bytes 1572872 | tf_op jit(solution)/shard_map/ppermute | solution.py:20
  558.8 11.9 %collective-permute-start.10 = (bf16[256,2,512]{0,2,1:T(8,128)(2,1)}, bf16[256,2,512]{0,2,1:T(8,128)(2,1)S(1)}, u32[]{:S(2)}, u32[]{:S(2)}) collective-permute-start(bf16[256,2,512]{0,2,1:T(8,128)(2,1)} %collective-permute-done.9), channel_id=1, source_target_pairs={{254,0},{0,2},{2,4},{4,6},{6,8},{8,10},{10,12},{12,14},{14,16},{16... | collective-permute-start | bytes 1572872 | tf_op jit(solution)/shard_map/ppermute | solution.py:20
  565.8 11.6 %collective-permute-start.14 = (bf16[256,2,512]{0,2,1:T(8,128)(2,1)S(1)}, bf16[256,2,512]{0,2,1:T(8,128)(2,1)S(1)}, u32[]{:S(2)}, u32[]{:S(2)}) collective-permute-start(bf16[256,2,512]{0,2,1:T(8,128)(2,1)S(1)} %collective-permute-done.13), channel_id=1, source_target_pairs={{2,0},{4,2},{6,4},{8,6},{10,8},{12,10},{14,12},{16,14},{18,16},{20... | collective-permute-start | bytes 1572872 | tf_op jit(solution)/shard_map/ppermute | solution.py:20
  570.7 11.9 %collective-permute-start.11 = (bf16[256,2,512]{0,2,1:T(8,128)(2,1)S(1)}, bf16[256,2,512]{0,2,1:T(8,128)(2,1)S(1)}, u32[]{:S(2)}, u32[]{:S(2)}) collective-permute-start(bf16[256,2,512]{0,2,1:T(8,128)(2,1)S(1)} %collective-permute-done.10), channel_id=1, source_target_pairs={{254,0},{0,2},{2,4},{4,6},{6,8},{8,10},{10,12},{12,14},{14,16},{16... | collective-permute-start | bytes 1572872 | tf_op jit(solution)/shard_map/ppermute | solution.py:20
  577.3 15.5 %collective-permute-start.15 = (bf16[256,2,512]{0,2,1:T(8,128)(2,1)S(1)}, bf16[256,2,512]{0,2,1:T(8,128)(2,1)S(1)}, u32[]{:S(2)}, u32[]{:S(2)}) collective-permute-start(bf16[256,2,512]{0,2,1:T(8,128)(2,1)S(1)} %collective-permute-done.14), channel_id=1, source_target_pairs={{2,0},{4,2},{6,4},{8,6},{10,8},{12,10},{14,12},{16,14},{18,16},{20... | collective-permute-start | bytes 1572872 | tf_op jit(solution)/shard_map/ppermute | solution.py:20
  (10 other events, 38.4 us)
Sparse Core Ops, SparseCore 0:
  59.4 223.7 all-gather.2
  298.7 24.9 reduce-scatter.2
  325.8 213.3 all-gather.4
  636.9 33.9 reduce-scatter.4
where the time goes:
time: 692 us; the launch traced here: 680 us
  waiting for transfers between devices  410 us (59%)
  local copies, waits for them, and re-layouts  142 us (21%)
  starting transfers between devices  40.8 us (6%)
  matrix products  38.6 us (6%)
  blocking collectives  20.6 us (3%)
  between operations  16.4 us (2%)
  other arithmetic  11.7 us (2%)
    all_gather x2, waiting for transfers between devices, on_device(): guide_pair = lax.all_gather(guide_pairs[step], 'seq', axis=0, tiled=True)  336 us
    reduce_scatter x2, waiting for transfers between devices, on_device(): lax.psum_scatter(partial_value, 'head', scatter_dimension=1, tiled=True)  54 us
    ppermute x16, starting transfers between devices, passed_along(): return lax.ppermute(block, axis, route)  40.6 us
    unnamed x49, local copies, waits for them, and re-layouts  37.1 us
    gather x4, local copies, waits for them, and re-layouts, on_device(): chosen = window_blocks[window_index]  25.1 us
    all_gather x2, blocking collectives, on_device(): whole = lax.all_gather(state, 'head', axis=1, tiled=True)  20.6 us
    ppermute x16, waiting for transfers between devices, passed_along(): return lax.ppermute(block, axis, route)  19.5 us
    reshape x2, local copies, waits for them, and re-layouts, on_device(): chosen = chosen.reshape(block_count, MAXK * BLOCK, 2, local_heads, HEAD_DIM)  16 us
  transfers between devices with their start and end apart: 20, of which 11 were waited for; matrix products, arithmetic and copies ran while one was open for 17% of the time, Pallas kernels for 0%

commit v1 on v0

--- a/solution.py
+++ b/solution.py
@@ -68,15 +68,11 @@
     local_heads = local_width // HEAD_DIM
     block_count = token_count // BLOCK
     scale = 1.0 / math.sqrt(HEAD_DIM)
-    home = position * block_count + jnp.arange(block_count, dtype=jnp.int32)[:, None]
-    valid = block_lists >= 0
-    entries = jnp.where(valid, block_lists, home)
-    source = entries // block_count
-    within = entries % block_count
-    offset = (source - position) % cycle_size
-    slot = (offset + ROW) % cycle_size
-    window_index = slot * block_count + within
-    live = jnp.repeat(valid, BLOCK, axis=1)
+    moves = jnp.array([-ROW, -1, 0, 1, ROW], dtype=jnp.int32)
+    tiles = (position + moves) % cycle_size
+    names = tiles[:, None] * block_count + jnp.arange(block_count, dtype=jnp.int32)
+    listed = jnp.any(block_lists[:, :, None] == names.reshape(-1), axis=1)
+    live = jnp.repeat(listed, BLOCK, axis=1)
     self_flat = self_weight.reshape(D, 3 * local_width)
     cross_pair_weight = cross_weight[:, 1:3].reshape(D, 2 * local_width)
     cross_query_weight = cross_weight[:, 0]
@@ -103,23 +99,21 @@
         projected = projected.reshape(token_count, 3, local_width)
         query = projected[:, 0]
         pair = projected[:, 1:3]
-        lower_side = []
-        upper_side = []
-        going_up = pair
-        going_down = pair
-        for hop in range(ROW):
-            going_up = passed_along(going_up, "seq", 1)
-            going_down = passed_along(going_down, "seq", -1)
-            lower_side.append(going_up)
-            upper_side.append(going_down)
-        window = jnp.concatenate(lower_side[::-1] + [pair] + upper_side, axis=0)
-        window_blocks = window.reshape(-1, BLOCK, 2, local_width)
-        chosen = window_blocks[window_index]
-        chosen = chosen.reshape(block_count, MAXK * BLOCK, 2, local_heads, HEAD_DIM)
+        window = jnp.concatenate(
+            [
+                passed_along(pair, "seq", ROW),
+                passed_along(pair, "seq", 1),
+                pair,
+                passed_along(pair, "seq", -1),
+                passed_along(pair, "seq", -ROW),
+            ],
+            axis=0,
+        )
+        window = window.reshape(-1, 2, local_heads, HEAD_DIM)
         queries = query.reshape(block_count, BLOCK, local_heads, HEAD_DIM)
         scores = (
             jnp.einsum(
-                "bqhd,bkhd->bhqk", queries, chosen[:, :, 0], preferred_element_type=jnp.float32
+                "bqhd,khd->bhqk", queries, window[:, 0], preferred_element_type=jnp.float32
             )
             * scale
         )
@@ -129,7 +123,7 @@
         total = jnp.sum(weights, axis=-1)
         rounded = weights.astype(jnp.bfloat16)
         mixed = jnp.einsum(
-            "bhqk,bkhd->bqhd", rounded, chosen[:, :, 1], preferred_element_type=jnp.float32
+            "bhqk,khd->bqhd", rounded, window[:, 1], preferred_element_type=jnp.float32
         )
         mixed = mixed / jnp.transpose(total, (0, 2, 1))[:, :, :, None]
         attended = mixed.reshape(token_count, local_width).astype(jnp.bfloat16)

time: 692 us -> 570 us (0.82)
  local copies, waits for them, and re-layouts: 142 us -> 47.3 us
  starting transfers between devices: 40.8 us -> 14.1 us
    ppermute x16 -> x8, starting transfers between devices: 40.6 us -> 13.6 us  [passed_along(): return lax.ppermute(block, axis, route)]
    reshape x4 -> x0, local copies, waits for them, and re-layouts: 25.9 us -> none  [the longest x2 16 us: on_device(): chosen = chosen.reshape(block_count, MAXK * BLOCK, 2, local_heads, HEAD_DIM)]
    gather x4 -> x0, local copies, waits for them, and re-layouts: 25.1 us -> none  [on_device(): chosen = window_blocks[window_index]]
    unnamed x49 -> x47, local copies, waits for them, and re-layouts: 37.1 us -> 18 us
    all_gather x2, waiting for transfers between devices: 336 us -> 351 us  [on_device(): guide_pair = lax.all_gather(guide_pairs[step], 'seq', axis=0, tiled=True)]
    concatenate x4 -> x2, local copies, waits for them, and re-layouts: 15.1 us -> 2.15 us  [on_device(): jnp.concatenate([passed_along(pair, 'seq', ROW), passed_along(pair, 'seq'...]
    ppermute x16 -> x8, waiting for transfers between devices: 19.5 us -> 7 us  [passed_along(): return lax.ppermute(block, axis, route)]
    slice x2 -> x0, local copies, waits for them, and re-layouts: 7.78 us -> none  [on_device(): chosen[:, :, 1]]
  transfers between devices with their start and end apart: 20 -> 12, of which waited for: 11 -> 8; matrix products, arithmetic and copies ran while one was open for 17% -> 13% of each run, Pallas kernels for 0% -> 0%
where the time goes in v1:
time: 570 us; the launch traced here: 561 us
  waiting for transfers between devices  408 us (72%)
  local copies, waits for them, and re-layouts  47.3 us (8%)
  matrix products  41.1 us (7%)
  blocking collectives  20.4 us (4%)
  between operations  16.4 us (3%)
  starting transfers between devices  14.1 us (2%)
  other arithmetic  13.6 us (2%)
    all_gather x2, waiting for transfers between devices, on_device(): guide_pair = lax.all_gather(guide_pairs[step], 'seq', axis=0, tiled=True)  351 us
    reduce_scatter x2, waiting for transfers between devices, on_device(): lax.psum_scatter(partial_value, 'head', scatter_dimension=1, tiled=True)  50.3 us
    all_gather x2, blocking collectives, on_device(): whole = lax.all_gather(state, 'head', axis=1, tiled=True)  20.4 us
    unnamed x47, local copies, waits for them, and re-layouts  18 us
    ppermute x8, starting transfers between devices, passed_along(): return lax.ppermute(block, axis, route)  13.6 us
  transfers between devices with their start and end apart: 12, of which 8 were waited for; matrix products, arithmetic and copies ran while one was open for 13% of the time, Pallas kernels for 0%

profile of v1, /device:TPU:32, one launch (start us, length us, event | category | flops | bytes accessed | tf_op | source)
XLA Modules:
  0.0 561.3 jit_solution(7443431622436207543)
XLA Ops:
  6.5 3.2 slice.102
  9.7 3.0 copy.61
  17.0 4.7 copy.39
  23.1 10.2 %all_gather.12 = bf16[256,1024]{1,0:T(8,128)(2,1)S(1)} all-gather(bf16[256,512]{1,0:T(8,128)(2,1)S(1)} %copy-done.6), channel_id=1, replica_groups=mesh['seq'=128,'head'=2] {'head'}, dimensions={1}, use_global_device_ids=true | all-gather | bytes 786432 | tf_op jit(solution)/shard_map/all_gather | solution.py:92
  34.2 4.0 convolution_convert_fusion.1
  44.0 4.8 collective-permute-start.2
  49.2 2.9 convolution_convert_fusion.4
  52.3 2.6 convolution_convert_fusion.3
  61.5 2.7 collective-permute-done.1
  68.6 2.5 fusion.4
  73.6 2.6 fusion.65
  78.0 153.4 %all-gather.3.cloned.1.call-done = bf16[1024,2,512]{2,0,1:T(8,128)(2,1)} async-done(((bf16[8,2,512]{2,0,1:T(8,128)(2,1)}), bf16[1024,2,512]{2,0,1:T(8,128)(2,1)}) %all-gather.3.cloned.1.call-update) | async-done | bytes 2097168 | tf_op jit(solution)/shard_map/all_gather | solution.py:130
  231.3 3.1 fusion.150
  239.0 2.7 multiply_reduce_fusion.1
  248.7 197.6 %all-gather.5.cloned.1.call-done = bf16[1024,2,512]{2,0,1:T(8,128)(2,1)} async-done(((bf16[8,2,512]{2,0,1:T(8,128)(2,1)}), bf16[1024,2,512]{2,0,1:T(8,128)(2,1)}) %all-gather.5.cloned.1.call-update) | async-done | bytes 2097168 | tf_op jit(solution)/shard_map/all_gather | solution.py:130
  450.7 22.7 %reduce-scatter.3.cloned.1.call-done = f32[256,512]{1,0:T(8,128)} async-done(((f32[256,1024]{1,0:T(8,128)}), f32[256,512]{1,0:T(8,128)}) %reduce-scatter.3.cloned.1.call-update) | async-done | bytes 524304 | tf_op jit(solution)/shard_map/reduce_scatter | solution.py:157
  474.8 10.2 %all_gather.14 = bf16[256,1024]{1,0:T(8,128)(2,1)S(1)} all-gather(bf16[256,512]{1,0:T(8,128)(2,1)S(1)} %fusion.84), channel_id=1, replica_groups=mesh['seq'=128,'head'=2] {'head'}, dimensions={1}, use_global_device_ids=true | all-gather | bytes 786432 | tf_op jit(solution)/shard_map/all_gather | solution.py:92
  485.5 3.0 convolution_convert_fusion
  491.0 4.8 collective-permute-start.6
  498.2 2.6 multiply_reduce_fusion
  502.6 2.6 fusion.71
  514.0 2.5 fusion.5
  519.0 2.6 fusion.59
  524.6 27.6 %reduce-scatter.5.cloned.1.call-done = f32[256,512]{1,0:T(8,128)} async-done(((f32[256,1024]{1,0:T(8,128)}), f32[256,512]{1,0:T(8,128)}) %reduce-scatter.5.cloned.1.call-update) | async-done | bytes 524304 | tf_op jit(solution)/shard_map/reduce_scatter | solution.py:157
  (127 shorter events, 66.4 us)
Async XLA Ops:
  6.5 70.0 %copy-start = (bf16[512,1024]{1,0:T(8,128)(2,1)S(1)}, bf16[512,1024]{1,0:T(8,128)(2,1)}, u32[]{:S(2)}) copy-start(bf16[512,1024]{1,0:T(8,128)(2,1)} %param.20) | copy-start | bytes 3145732
  6.5 6.2 %copy-start.10 = (bf16[2,8,1024]{2,1,0:T(8,128)(2,1)S(1)}, bf16[2,8,1024]{2,1,0:T(8,128)(2,1)}, u32[]{:S(2)}) copy-start(bf16[2,8,1024]{2,1,0:T(8,128)(2,1)} %param.17) | copy-start | bytes 98308
  6.5 224.8 %all-gather.3.cloned.1.call-start = ((), (), s32[]{:S(2)}) async-start(), calls=%async_computation.2 | async-start | bytes 2113536 | tf_op jit(solution)/shard_map/all_gather | solution.py:130
  14.4 431.9 %all-gather.5.cloned.1.call-start = ((), (), s32[]{:S(2)}) async-start(), calls=%async_computation.4 | async-start | bytes 2113536 | tf_op jit(solution)/shard_map/all_gather | solution.py:130
  16.9 4.8 copy-start.13
  16.9 6.1 %copy-start.6 = (bf16[256,512]{1,0:T(8,128)(2,1)S(1)}, bf16[256,512]{1,0:T(8,128)(2,1)}, u32[]{:S(2)}) copy-start(bf16[256,512]{1,0:T(8,128)(2,1)} %param.12) | copy-start | bytes 786436
  38.1 16.7 %copy-start.16 = (s32[5]{0:T(128)S(1)}, s32[5]{0:T(128)}, u32[]{:S(2)}) copy-start(s32[5]{0:T(128)} %constant.85.clone) | copy-start | bytes 64
  38.1 16.9 %copy-start.14 = (s32[2,6]{1,0:T(2,128)S(1)}, s32[2,6]{1,0:T(2,128)}, u32[]{:S(2)}) copy-start(s32[2,6]{1,0:T(2,128)} %param.16) | copy-start | bytes 148
  42.4 18.0 %collective-permute-start = (bf16[256,2,512]{0,2,1:T(8,128)(2,1)}, bf16[256,2,512]{0,2,1:T(8,128)(2,1)}, u32[]{:S(2)}, u32[]{:S(2)}) collective-permute-start(bf16[256,2,512]{0,2,1:T(8,128)(2,1)} %slice.120), channel_id=1, source_target_pairs={{248,0},{250,2},{252,4},{254,6},{0,8},{2,10},{4,12},{6,14},{8,16},... | collective-permute-start | bytes 1572872 | tf_op jit(solution)/shard_map/ppermute | solution.py:20
  44.0 20.3 %collective-permute-start.1 = (bf16[256,2,512]{0,2,1:T(8,128)(2,1)}, bf16[256,2,512]{0,2,1:T(8,128)(2,1)}, u32[]{:S(2)}, u32[]{:S(2)}) collective-permute-start(bf16[256,2,512]{0,2,1:T(8,128)(2,1)} %slice.120), channel_id=1, source_target_pairs={{254,0},{0,2},{2,4},{4,6},{6,8},{8,10},{10,12},{12,14},{14,16},{16... | collective-permute-start | bytes 1572872 | tf_op jit(solution)/shard_map/ppermute | solution.py:20
  44.0 22.4 %collective-permute-start.2 = (bf16[256,2,512]{0,2,1:T(8,128)(2,1)}, bf16[256,2,512]{0,2,1:T(8,128)(2,1)}, u32[]{:S(2)}, u32[]{:S(2)}) collective-permute-start(bf16[256,2,512]{0,2,1:T(8,128)(2,1)} %slice.120), channel_id=1, source_target_pairs={{2,0},{4,2},{6,4},{8,6},{10,8},{12,10},{14,12},{16,14},{18,16},{20... | collective-permute-start | bytes 1572872 | tf_op jit(solution)/shard_map/ppermute | solution.py:20
  48.7 18.8 %collective-permute-start.3 = (bf16[256,2,512]{0,2,1:T(8,128)(2,1)}, bf16[256,2,512]{0,2,1:T(8,128)(2,1)}, u32[]{:S(2)}, u32[]{:S(2)}) collective-permute-start(bf16[256,2,512]{0,2,1:T(8,128)(2,1)} %slice.120), channel_id=1, source_target_pairs={{8,0},{10,2},{12,4},{14,6},{16,8},{18,10},{20,12},{22,14},{24,16},... | collective-permute-start | bytes 1572872 | tf_op jit(solution)/shard_map/ppermute | solution.py:20
  52.0 421.4 %reduce-scatter.3.cloned.1.call-start = ((), (), s32[]{:S(2)}) async-start(), calls=%async_computation.3 | async-start | bytes 1572864 | tf_op jit(solution)/shard_map/reduce_scatter | solution.py:157
  60.4 8.2 %copy-start.11 = (bf16[2,128,8,64]{1,0,3,2:T(2,128)(2,1)S(1)}, bf16[2,128,8,64]{1,0,3,2:T(2,128)(2,1)}, u32[]{:S(2)}) copy-start(bf16[2,128,8,64]{1,0,3,2:T(2,128)(2,1)} %reshape_squeeze.18) | copy-start | bytes 786436
  243.5 2.0 copy-start.3
  245.5 2.8 copy-start.15
  247.0 305.3 %reduce-scatter.5.cloned.1.call-start = ((), (), s32[]{:S(2)}) async-start(), calls=%async_computation.5 | async-start | bytes 1572864 | tf_op jit(solution)/shard_map/reduce_scatter | solution.py:157
  474.8 10.7 %copy-start.7 = (bf16[256,512]{1,0:T(8,128)(2,1)}, bf16[256,512]{1,0:T(8,128)(2,1)S(1)}, u32[]{:S(2)}) copy-start(bf16[256,512]{1,0:T(8,128)(2,1)S(1)} %fusion.84) | copy-start | bytes 786436
  489.5 17.7 %collective-permute-start.4 = (bf16[256,2,512]{0,2,1:T(8,128)(2,1)}, bf16[256,2,512]{0,2,1:T(8,128)(2,1)}, u32[]{:S(2)}, u32[]{:S(2)}) collective-permute-start(bf16[256,2,512]{0,2,1:T(8,128)(2,1)} %slice.130), channel_id=1, source_target_pairs={{248,0},{250,2},{252,4},{254,6},{0,8},{2,10},{4,12},{6,14},{8,16},... | collective-permute-start | bytes 1572872 | tf_op jit(solution)/shard_map/ppermute | solution.py:20
  491.0 19.4 %collective-permute-start.5 = (bf16[256,2,512]{0,2,1:T(8,128)(2,1)}, bf16[256,2,512]{0,2,1:T(8,128)(2,1)}, u32[]{:S(2)}, u32[]{:S(2)}) collective-permute-start(bf16[256,2,512]{0,2,1:T(8,128)(2,1)} %slice.130), channel_id=1, source_target_pairs={{254,0},{0,2},{2,4},{4,6},{6,8},{8,10},{10,12},{12,14},{14,16},{16... | collective-permute-start | bytes 1572872 | tf_op jit(solution)/shard_map/ppermute | solution.py:20
  491.0 20.5 %collective-permute-start.6 = (bf16[256,2,512]{0,2,1:T(8,128)(2,1)}, bf16[256,2,512]{0,2,1:T(8,128)(2,1)}, u32[]{:S(2)}, u32[]{:S(2)}) collective-permute-start(bf16[256,2,512]{0,2,1:T(8,128)(2,1)} %slice.130), channel_id=1, source_target_pairs={{2,0},{4,2},{6,4},{8,6},{10,8},{12,10},{14,12},{16,14},{18,16},{20... | collective-permute-start | bytes 1572872 | tf_op jit(solution)/shard_map/ppermute | solution.py:20
  495.8 17.1 %collective-permute-start.7 = (bf16[256,2,512]{0,2,1:T(8,128)(2,1)}, bf16[256,2,512]{0,2,1:T(8,128)(2,1)}, u32[]{:S(2)}, u32[]{:S(2)}) collective-permute-start(bf16[256,2,512]{0,2,1:T(8,128)(2,1)} %slice.130), channel_id=1, source_target_pairs={{8,0},{10,2},{12,4},{14,6},{16,8},{18,10},{20,12},{22,14},{24,16},... | collective-permute-start | bytes 1572872 | tf_op jit(solution)/shard_map/ppermute | solution.py:20
  518.9 3.4 copy-start.5
  518.9 3.4 copy-start.12
  (5 other events, 8.3 us)
Sparse Core Ops, SparseCore 0:
  14.5 216.7 all-gather.2
  233.2 213.0 all-gather.4
  448.8 24.5 reduce-scatter.2
  524.0 28.2 reduce-scatter.4

commit v2 on v1

v2 whole, which is shorter than its diff:
```python
import functools
import math

import jax
import jax.numpy as jnp
from jax import lax
from jax.experimental import pallas as pl
from jax.experimental.pallas import tpu as pltpu
from jax.sharding import PartitionSpec as P

D = 1024
HALF = 512
HEAD_DIM = 64
FREQ = 256
BLOCK = 128
TOK = 256
STEPS = 2
NSEQ = 128
GUIDE = 8
MESH = pl.DeviceIdType.MESH
F32 = jnp.float32
BF16 = jnp.bfloat16
OWN, CORE, UP, DOWN, OVER = range(5)


def signal_level(moment):
    angle = (moment.astype(F32) / 1000.0 + 0.008) / 1.008 * (math.pi / 2.0)
    cosine = jnp.cos(angle)
    return cosine * cosine


def places(s):
    q = lax.rem(s, 4)
    wrap = lambda v: lax.rem(v + NSEQ, NSEQ)
    turn = lambda d: 16 * (s // 16) + lax.rem(lax.rem(s, 16) + 4 * d, 16)
    return dict(
        core=s + 1 - 2 * lax.rem(s, 2),
        over=4 * (s // 4) + 3 - q,
        diag=4 * (s // 4) + lax.rem(q + 2, 4),
        up=wrap(s + 4),
        down=wrap(s - 4),
        turn1=turn(1),
        turn2=turn(2),
        turn3=turn(3),
        zup=wrap(s + 16),
        zdown=wrap(s - 16),
    )


def norm(parts):
    width = sum(p.shape[1] for p in parts)
    mean = sum(jnp.sum(p, axis=1, keepdims=True) for p in parts) * (1.0 / width)
    parts = [p - mean for p in parts]
    var = sum(jnp.sum(p * p, axis=1, keepdims=True) for p in parts) * (1.0 / width)
    scale = lax.rsqrt(var + 1e-06)
    return [p * scale for p in parts]


def kernel(
    active, coef, mask, bias, guid, lat, known, mw, sw, sow, cw, cow,
    out,
    latv, knownv, statev, mwv, swv, sowv, cwv, cowv, tab, mixb, plainb, kvb, gb, ab,
    qs, cqs, acc, mx, att, gud, part, psend, precv, pfin,
    lsem, hs, hr, kss, krs, kvs, kvr, gas, gar, gbs, gbr, zs, zr, cs, cr, ps, pr,
):
    s = lax.axis_index("seq")
    h = lax.axis_index("head")
    q = lax.rem(s, 4)
    c = lax.rem(s, 2)
    at = places(s)
    to = {k: {"seq": v, "head": h} for k, v in at.items()}
    to["head"] = {"seq": s, "head": 1 - h}

    loads = [
        (cw.at[1], cwv.at[1]),
        (cw.at[2], cwv.at[2]),
        (lat, latv.at[h]),
        (sw.at[1], swv.at[1]),
        (sw.at[2], swv.at[2]),
        (mw, mwv),
        (sw.at[0], swv.at[0]),
        (cw.at[0], cwv.at[0]),
        (sow, sowv),
        (cow, cowv),
        (known, knownv.at[h]),
    ]
    loads = [pltpu.make_async_copy(a, b, lsem.at[n]) for n, (a, b) in enumerate(loads)]
    for load in loads:
        load.start()

    barrier = pltpu.get_barrier_semaphore()
    for place in to.values():
        pl.semaphore_signal(barrier, inc=1, device_id=place, device_id_type=MESH)
    pl.semaphore_wait(barrier, len(to))

    def remote(src, dst, send, recv, place):
        return pltpu.make_async_remote_copy(
            src_ref=src, dst_ref=dst, send_sem=send, recv_sem=recv,
            device_id=to[place], device_id_type=MESH,
        )

    sent = []

    def send(*args):
        copy = remote(*args)
        copy.start()
        sent.append(copy)

    def rows(b):
        return pl.ds(BLOCK * b, BLOCK)

    for b in range(2):
        send(lat.at[rows(b)], latv.at[h, rows(b)], hs.at[b], hr.at[b], "head")

    loads[0].wait()
    loads[1].wait()
    guide_in = norm([guid[...].astype(F32)])[0].astype(BF16)
    for j in range(2):
        ab[q, :, HALF * j : HALF * (j + 1)] = jnp.dot(
            guide_in, cwv[j + 1], preferred_element_type=F32
        ).astype(BF16)
    for n, place in enumerate(("core", "over", "diag")):
        send(ab.at[q], ab.at[q], gas.at[n], gar.at[n], place)

    loads[5].wait()

    def modulate(k, sums):
        row = mwv[k].astype(F32)
        return sums[0] + active[0, k] * row, sums[1] + active[1, k] * row

    zero = jnp.zeros((4, D), F32)
    tab[0], tab[1] = lax.fori_loop(0, FREQ, modulate, (zero, zero), unroll=4)

    def guide_second():
        for n, place in enumerate(("core", "over", "diag")):
            remote(ab.at[q], ab.at[q], gas.at[n], gar.at[n], place).wait_recv()
        lanes = pl.ds(pl.multiple_of(HALF * c, HALF), HALF)
        own = [ab[k, :, lanes].astype(F32) for k in range(4)]
        for i in range(STEPS):
            gb[c, i, 0, 0:32, :] = jnp.concatenate(
                [o[GUIDE * i : GUIDE * (i + 1)] for o in own], axis=0
            ).astype(BF16)
            for d in range(1, 4):
                send(
                    gb.at[c, i, 0, 0:32], gb.at[c, i, 0, 32 * d : 32 * d + 32],
                    gbs.at[i, d - 1], gbr.at[i, d - 1], f"turn{d}",
                )

    def ring(i, src, dst):
        send(gb.at[c, i, src], gb.at[c, i, dst], zs.at[i, dst], zr.at[i, dst],
             "zup" if dst in (1, 3, 5) else "zdown")

    def across(i, slot):
        send(gb.at[c, i, slot], gb.at[c, i, slot], cs.at[i, slot], cr.at[i, slot], "core")

    def guide_third(i):
        for d in range(1, 4):
            remote(
                gb.at[c, i, 0, 0:32], gb.at[c, i, 0, 32 * d : 32 * d + 32],
                gbs.at[i, d - 1], gbr.at[i, d - 1], f"turn{d}",
            ).wait_recv()
        ring(i, 0, 1)
        ring(i, 0, 2)
        across(i, 0)

    onward = {1: 3, 2: 4, 3: 5, 4: 6, 6: 7}

    def hop(i, *slots):
        for slot in slots:
            remote(gb.at[c, i, 0], gb.at[c, i, slot], zs.at[i, slot], zr.at[i, slot],
                   "zup").wait_recv()
            if slot in onward:
                ring(i, slot, onward[slot])
            across(i, slot)

    lane = lax.broadcasted_iota(jnp.int32, (1, BLOCK), 1)
    low = jnp.where(lane < HEAD_DIM, 1.0, 0.0).astype(BF16)
    low_f = lax.broadcasted_iota(jnp.int32, (TOK, BLOCK), 1) < HEAD_DIM
    high = (1.0 - low.astype(F32)).astype(BF16)

    def normalize(b, state):
        r = rows(b)
        normed = norm([state[0, r].astype(F32), state[1, r].astype(F32)])
        return r, normed

    def mix(i, b, state):
        r, normed = normalize(b, state)
        for n in range(2):
            cols = slice(HALF * n, HALF * (n + 1))
            mixb[r, cols] = (normed[n] * (1.0 + tab[i, 1:2, cols]) + tab[i, 0:1, cols]).astype(BF16)
            plainb[r, cols] = normed[n].astype(BF16)

    def keys_values(i, b):
        r = rows(b)
        x = mixb[r, :]
        for j in range(2):

            def tile(t, _):
                w = swv[1 + j, :, pl.ds(pl.multiple_of(256 * t, 256), 256)]
                kvb[i, OWN, r, pl.ds(pl.multiple_of(HALF * j + 256 * t, 256), 256)] = jnp.dot(
                    x, w, preferred_element_type=F32
                ).astype(BF16)
                return 0

            lax.fori_loop(0, 2, tile, 0)
        for n, (slot, place) in enumerate(((CORE, "core"), (DOWN, "up"), (UP, "down"))):
            send(kvb.at[i, OWN, r], kvb.at[i, slot, r], kvs.at[i, n, b], kvr.at[i, slot, b], place)

        @pl.when(q * (3 - q) > 0)
        def _():
            remote(kvb.at[i, OWN, r], kvb.at[i, OVER, r], kvs.at[i, 3, b], kvr.at[i, OVER, b], "over").start()

        sent.append(remote(kvb.at[i, OWN, r], kvb.at[i, OVER, r], kvs.at[i, 3, b], kvr.at[i, OVER, b], "over"))

    def arrived(i, slot, b):
        remote(kvb.at[i, OWN, rows(b)], kvb.at[i, slot, rows(b)], kvs.at[i, 0, b],
               kvr.at[i, slot, b], "core").wait_recv()

    def relay(i, b):
        arrived(i, UP, b)
        arrived(i, DOWN, b)
        r = rows(b)

        @pl.when(q * (3 - q) == 0)
        def _():
            remote(kvb.at[i, UP + q // 3, r], kvb.at[i, OVER, r], kvs.at[i, 3, b], kvr.at[i, OVER, b], "over").start()

    row_id = lax.broadcasted_iota(jnp.int32, (TOK, BLOCK), 0) // BLOCK
    lane_id = lax.broadcasted_iota(jnp.int32, (TOK, BLOCK), 1)

    def queries(x_ref, w_ref, dst, marked):
        def tile(t, _):
            w = w_ref[0, :, pl.ds(pl.multiple_of(256 * t, 256), 256)]
            y = jnp.dot(x_ref[...], w, preferred_element_type=F32)
            y = y.astype(BF16).astype(F32) * (1.0 / math.sqrt(HEAD_DIM))
            for u in range(2):
                z = y[:, BLOCK * u : BLOCK * (u + 1)]
                mark_a = jnp.where(lane_id == HEAD_DIM + row_id, 1.0, 0.0) if marked else 0.0
                mark_b = jnp.where(lane_id == row_id, 1.0, 0.0) if marked else 0.0
                dst[4 * t + 2 * u] = jnp.where(low_f, z, mark_a).astype(BF16)
                dst[4 * t + 2 * u + 1] = jnp.where(low_f, mark_b, z).astype(BF16)
            return 0

        lax.fori_loop(0, 2, tile, 0)

    def attend(q_ref, load, first, marks=None):
        keep = (low, high)

        def pair(p, _):
            k, v = load(pl.ds(pl.multiple_of(BLOCK * p, BLOCK), BLOCK))
            for u in range(2):
                head = 2 * p + u
                ku = k if marks is None else k * keep[u] + marks[u]
                vu = v * keep[u] + keep[1 - u]
                scores = lax.dot_general(
                    q_ref[head], ku, (((1,), (1,)), ((), ())), preferred_element_type=F32
                )
                peak = jnp.max(scores, axis=1, keepdims=True)
                if not first:
                    old = mx[head]
                    peak = jnp.maximum(peak, old[:, 0:1])
                weights = jnp.exp(scores - peak).astype(BF16)
                mixed = jnp.dot(weights, vu, preferred_element_type=F32)
                wide = jnp.broadcast_to(peak, (TOK, BLOCK))
                if not first:
                    mixed = mixed + acc[head] * jnp.exp(old - wide)
                acc[head] = mixed
                mx[head] = wide
            return 0

        lax.fori_loop(0, 4, pair, 0)

    def attend_tile(i, slot):
        marks = [
            jnp.concatenate(
                [jnp.broadcast_to(bias[u, 2 * slot + b : 2 * slot + b + 1, :], (BLOCK, BLOCK)) for b in range(2)],
                axis=0,
            ).astype(BF16)
            for u in range(2)
        ]

        def load(lanes):
            return kvb[i, slot, :, lanes], kvb[i, slot, :, pl.ds(HALF + lanes.start, BLOCK)]

        attend(qs, load, slot == OWN, marks)

    def attend_guide(i, n):
        def load(lanes):
            return [
                gb[j, i, 2 * n : 2 * n + 2, :, lanes].reshape(TOK, BLOCK) for j in range(2)
            ]

        attend(cqs, load, n == 0)

    def crossed(i, *slots):
        for slot in slots:
            remote(gb.at[c, i, 0], gb.at[1 - c, i, slot], cs.at[i, slot], cr.at[i, slot],
                   "core").wait_recv()

    def finish(dst):
        def pair(p, _):
            a, b = acc[2 * p], acc[2 * p + 1]
            a = a / pltpu.roll(a, HEAD_DIM, 1)
            b = b / pltpu.roll(b, HEAD_DIM, 1)
            dst[:, pl.ds(pl.multiple_of(BLOCK * p, BLOCK), BLOCK)] = jnp.where(low_f, a, b).astype(BF16)
            return 0

        lax.fori_loop(0, 4, pair, 0)

    def project(i, b, x_ref, w_ref, gate, first):
        r = rows(b)
        x = x_ref[r, :]

        def tile(t, _):
            cols = pl.ds(pl.multiple_of(256 * t, 256), 256)
            y = jnp.dot(x, w_ref[:, cols], preferred_element_type=F32) * tab[i, gate : gate + 1, cols]
            y = y if first else y + part[r, cols]
            part[r, cols] = y
            if not first:
                psend[i, r, cols] = y.astype(BF16)
            return 0

        lax.fori_loop(0, 4, tile, 0)

    def seam(b):
        flags = jnp.broadcast_to(mask[b : b + 1, :], (BLOCK, BLOCK))
        wide = jnp.transpose(flags)
        return jnp.concatenate([wide] * 4, axis=1) > 0.5

    def updated(i, b, n, state, noise):
        r = rows(b)
        moved = coef[4 * i] * state + coef[4 * i + 1] * noise
        kept = coef[4 * i + 2] * knownv[n, r].astype(F32) + coef[4 * i + 3] * latv[n, r].astype(F32)
        return jnp.where(seam(b), moved, kept).astype(BF16)

    loads[2].wait()
    loads[3].wait()
    loads[4].wait()
    for b in range(2):
        remote(lat.at[rows(b)], latv.at[1 - h, rows(b)], hs.at[b], hr.at[b], "head").wait_recv()
        mix(0, b, latv)
        keys_values(0, b)
        if b == 0:
            guide_second()
    loads[6].wait()
    loads[7].wait()
    send(known, knownv.at[h], kss.at[0], krs.at[0], "head")
    queries(mixb, swv, qs, True)
    queries(plainb, cwv, cqs, False)
    guide_third(0)
    guide_third(1)
    attend_tile(0, OWN)
    hop(0, 1, 2)
    relay(0, 0)
    arrived(0, CORE, 0)
    arrived(0, CORE, 1)
    attend_tile(0, CORE)
    hop(1, 1, 2)
    hop(0, 3, 4)
    relay(0, 1)
    attend_tile(0, UP)
    hop(0, 5, 6)
    hop(1, 3, 4)
    attend_tile(0, DOWN)
    hop(0, 7)
    hop(1, 5, 6)
    arrived(0, OVER, 0)
    arrived(0, OVER, 1)
    attend_tile(0, OVER)
    hop(1, 7)
    finish(att)
    for n in range(4):
        crossed(0, 2 * n, 2 * n + 1)
        attend_guide(0, n)
    finish(gud)
    loads[8].wait()
    loads[9].wait()
    for b in range(2):
        project(0, b, att, sowv, 2, True)
        project(0, b, gud, cowv, 3, False)
        send(psend.at[0, rows(b)], precv.at[rows(b)], ps.at[0, b], pr.at[0, b], "head")

    loads[10].wait()
    remote(known, knownv.at[1 - h], kss.at[0], krs.at[0], "head").wait_recv()
    for b in range(2):
        r = rows(b)
        remote(psend.at[0, r], precv.at[r], ps.at[0, b], pr.at[0, b], "head").wait_recv()
        for n in range(2):
            cols = slice(HALF * n, HALF * (n + 1))
            noise = part[r, cols] + precv[r, cols].astype(F32)
            statev[n, r] = updated(0, b, n, latv[n, r].astype(F32), noise)
        mix(1, b, statev)
        keys_values(1, b)
    queries(plainb, cwv, cqs, False)
    queries(mixb, swv, qs, True)
    crossed(1, *range(8))
    attend_guide(1, 0)
    attend_guide(1, 1)
    relay(1, 0)
    attend_guide(1, 2)
    attend_guide(1, 3)
    relay(1, 1)
    finish(gud)
    for b in range(2):
        project(1, b, gud, cowv, 3, True)
    attend_tile(1, OWN)
    arrived(1, CORE, 0)
    arrived(1, CORE, 1)
    attend_tile(1, CORE)
    attend_tile(1, UP)
    attend_tile(1, DOWN)
    arrived(1, OVER, 0)
    arrived(1, OVER, 1)
    attend_tile(1, OVER)
    finish(att)
    mine = pl.ds(pl.multiple_of(HALF * h, HALF), HALF)
    theirs = pl.ds(pl.multiple_of(HALF * (1 - h), HALF), HALF)
    for b in range(2):
        project(1, b, att, sowv, 2, False)
        send(psend.at[1, rows(b), theirs], pfin.at[rows(b)], ps.at[1, b], pr.at[1, b], "head")
    for b in range(2):
        r = rows(b)
        remote(psend.at[1, r, theirs], pfin.at[r], ps.at[1, b], pr.at[1, b], "head").wait_recv()
        noise = part[r, mine] + pfin[r].astype(F32)
        out[r] = updated(1, b, h, statev[h, r].astype(F32), noise)

    for copy in sent:
        copy.wait_send()


def on_device(
    latents, known, seam_mask, timesteps, block_lists, guidance,
    modulation_weight, self_weight, self_out_weight, cross_weight, cross_out_weight,
):
    s = lax.axis_index("seq")
    at = places(s)
    other = 2 * s - at["core"]
    names = jnp.stack([s, at["core"], at["up"], at["down"], lax.rem(other + NSEQ, NSEQ)])
    names = (2 * names[:, None] + jnp.arange(2)).reshape(-1)
    listed = jnp.any(block_lists[:, :, None] == names, axis=1)
    shut = jnp.where(listed, 0.0, -1e30).astype(F32)
    lanes = jnp.arange(BLOCK)
    bias = jnp.stack(
        [
            sum(jnp.where(lanes == base + b, shut[b][:, None], 0.0) for b in range(2))
            for base in (HEAD_DIM, 0)
        ]
    )
    half = FREQ // 2
    frequency = jnp.exp(-math.log(10000.0) * jnp.arange(half, dtype=F32) / half)
    phase = timesteps[:STEPS].astype(F32)[:, None] * frequency
    embed = jnp.concatenate([jnp.cos(phase), jnp.sin(phase)], axis=1)
    active = jax.nn.silu(embed).astype(BF16).astype(F32)
    level = signal_level(timesteps)
    root, rest = jnp.sqrt(level), jnp.sqrt(1.0 - level)
    ratio = root[1:] / root[:-1]
    coef = jnp.stack([ratio, rest[1:] - ratio * rest[:-1], root[1:], rest[1:]], axis=1)
    mask = seam_mask.astype(F32).reshape(2, BLOCK)
    vmem = pl.BlockSpec(memory_space=pltpu.VMEM)
    smem = pl.BlockSpec(memory_space=pltpu.SMEM)
    hbm = pl.BlockSpec(memory_space=pl.ANY)
    dma = lambda *shape: pltpu.SemaphoreType.DMA(shape)
    return pl.pallas_call(
        kernel,
        out_shape=jax.ShapeDtypeStruct((TOK, HALF), BF16),
        in_specs=[smem, smem, vmem, vmem, vmem] + [hbm] * 7,
        out_specs=vmem,
        scratch_shapes=[
            pltpu.VMEM((2, TOK, HALF), BF16),
            pltpu.VMEM((2, TOK, HALF), BF16),
            pltpu.VMEM((2, TOK, HALF), BF16),
            pltpu.VMEM((FREQ, 4, D), BF16),
            pltpu.VMEM((3, D, HALF), BF16),
            pltpu.VMEM((HALF, D), BF16),
            pltpu.VMEM((3, D, HALF), BF16),
            pltpu.VMEM((HALF, D), BF16),
            pltpu.VMEM((STEPS, 4, D), F32),
            pltpu.VMEM((TOK, D), BF16),
            pltpu.VMEM((TOK, D), BF16),
            pltpu.VMEM((STEPS, 5, TOK, D), BF16),
            pltpu.VMEM((2, STEPS, 8, BLOCK, HALF), BF16),
            pltpu.VMEM((4, STEPS * GUIDE, D), BF16),
            pltpu.VMEM((8, TOK, BLOCK), BF16),
            pltpu.VMEM((8, TOK, BLOCK), BF16),
            pltpu.VMEM((8, TOK, BLOCK), F32),
            pltpu.VMEM((8, TOK, BLOCK), F32),
            pltpu.VMEM((TOK, HALF), BF16),
            pltpu.VMEM((TOK, HALF), BF16),
            pltpu.VMEM((TOK, D), F32),
            pltpu.VMEM((STEPS, TOK, D), BF16),
            pltpu.VMEM((TOK, D), BF16),
            pltpu.VMEM((TOK, HALF), BF16),
            dma(11), dma(2), dma(2), dma(1), dma(1),
            dma(STEPS, 4, 2), dma(STEPS, 5, 2),
            dma(3), dma(3), dma(STEPS, 3), dma(STEPS, 3),
            dma(STEPS, 8), dma(STEPS, 8), dma(STEPS, 8), dma(STEPS, 8),
            dma(STEPS, 2), dma(STEPS, 2),
        ],
        compiler_params=pltpu.CompilerParams(
            collective_id=0, has_side_effects=True, vmem_limit_bytes=56 << 20
        ),
        name="denoise",
    )(
        active, coef.reshape(-1), mask, bias, guidance.reshape(STEPS * GUIDE, D),
        latents, known, modulation_weight, jnp.transpose(self_weight, (1, 0, 2)),
        self_out_weight, jnp.transpose(cross_weight, (1, 0, 2)), cross_out_weight,
    )


def solution(mesh):
    in_specs = (
        P("seq", "head"), P("seq", "head"), P("seq"), P(), P("seq", None), P(None, "seq", None),
        P(), P(None, None, "head"), P("head", None), P(None, None, "head"), P("head", None),
    )
    return jax.shard_map(
        on_device, mesh=mesh, in_specs=in_specs, out_specs=P("seq", "head"), check_vma=False
    )
```

time: 570 us -> 144 us (0.25); the launches traced: 561 us -> 142 us
  waiting for transfers between devices: 408 us -> 0 us
  Pallas kernels: 0 us -> 135 us
  local copies, waits for them, and re-layouts: 47.3 us -> 2.57 us
  matrix products: 41.1 us -> 0 us
  blocking collectives: 20.4 us -> 0 us
  between operations: 16.4 us -> 0.03 us
  starting transfers between devices: 14.1 us -> 0 us
  other arithmetic: 13.6 us -> 4.96 us
    all_gather x2 -> x0, waiting for transfers between devices: 351 us -> none  [on_device(): guide_pair = lax.all_gather(guide_pairs[step], 'seq', axis=0, tiled=True)]
    pallas_call x0 -> x1, Pallas kernels: none -> 135 us  [on_device(): pl.pallas_call(kernel, out_shape=jax.ShapeDtypeStruct((TOK, HALF), BF16),...]
    reduce_scatter x2 -> x0, waiting for transfers between devices: 50.3 us -> none  [on_device(): lax.psum_scatter(partial_value, 'head', scatter_dimension=1, tiled=True)]
    dot_general x20 -> x0, matrix products: 41.1 us -> none  [the longest x2 6.96 us: on_device(): jnp.dot(mixed_in, self_flat, preferred_element_type=jnp.float32)]
    all_gather x2 -> x0, blocking collectives: 20.4 us -> none  [on_device(): whole = lax.all_gather(state, 'head', axis=1, tiled=True)]
    slice x12 -> x1, local copies, waits for them, and re-layouts: 20.2 us -> 0.01 us  [on_device(): shut[b][:, None]]
    unnamed x47 -> x1, local copies, waits for them, and re-layouts: 18 us -> 1.67 us
    ppermute x8 -> x0, starting transfers between devices: 13.6 us -> none  [passed_along(): return lax.ppermute(block, axis, route)]
  transfers between devices with their start and end apart: 12 -> 0, of which waited for: 8 -> 0; matrix products, arithmetic and copies ran while one was open for 13% -> 0% of each run, Pallas kernels for 0% -> 0%
where the time goes in v2:
time: 144 us; the launch traced here: 142 us
  Pallas kernels  135 us (94%)
  other arithmetic  4.96 us (3%)
  local copies, waits for them, and re-layouts  2.57 us (2%)
    pallas_call x1, Pallas kernels, on_device(): pl.pallas_call(kernel, out_shape=jax.ShapeDtypeStruct((TOK, HALF), BF16),...  135 us

profile of v2, /device:TPU:32, one launch (start us, length us, event | category | flops | bytes accessed | tf_op | source)
XLA Modules:
  0.0 142.4 jit_solution(5962429321938867645)
XLA Ops:
  0.0 0.1 stack.48
  0.1 0.7 slice_convert_fusion
  0.8 1.2 convert_bitcast_fusion.mask
  2.0 0.1 multiply_cosine_fusion
  2.1 0.6 fusion.1.active
  2.7 0.7 fusion.2
  3.4 0.1 subtract_bitcast_fusion
  3.5 0.1 copy.14
  3.6 0.6 reshape.268.coef
  4.2 0.1 iota_add_fusion
  4.3 0.1 add.74
  4.4 0.8 compare_reduce_fusion
  5.2 0.1 select_add_fusion.1
  5.3 0.6 pad_maximum_fusion.bias
  5.9 134.9 %denoise.1 = bf16[256,512]{1,0:T(8,128)(2,1)} custom-call(f32[2,256]{1,0:T(2,128)} %fusion.1.active, f32[8]{0:T(128)} %reshape.268.coef, f32[2,128]{1,0:T(2,128)} %convert_bitcast_fusion.mask, f32[2,10,128]{2,1,0:T(8,128)} %pad_maximum_fusion.bias, bf16[16,1024]{1,0:T(8,128)(2,1)} %bitcast.23, bf16[256,512]{1,0:T(8,128)(2,1)} %lat.1, ...), custom_call_target="tpu_custom_call" | custom-call | tf_op jit(solution)/shard_map/denoise/pallas_call | solution.py:463
  140.8 1.7 %copy.16 = bf16[256,512]{1,0:T(8,128)(2,1)} copy(bf16[256,512]{1,0:T(8,128)(2,1)} %denoise.1) | data formatting | bytes 524288
  (7 shorter events, 0.1 us)

commit v3 on v2

--- a/solution.py
+++ b/solution.py
@@ -21,12 +21,6 @@
 F32 = jnp.float32
 BF16 = jnp.bfloat16
 OWN, CORE, UP, DOWN, OVER = range(5)
-
-
-def signal_level(moment):
-    angle = (moment.astype(F32) / 1000.0 + 0.008) / 1.008 * (math.pi / 2.0)
-    cosine = jnp.cos(angle)
-    return cosine * cosine
 
 
 def places(s):
@@ -57,10 +51,10 @@
 
 
 def kernel(
-    active, coef, mask, bias, guid, lat, known, mw, sw, sow, cw, cow,
+    steps, lists, mask, guid, lat, known, mw, sw, sow, cw, cow,
     out,
-    latv, knownv, statev, mwv, swv, sowv, cwv, cowv, tab, mixb, plainb, kvb, gb, ab,
-    qs, cqs, acc, mx, att, gud, part, psend, precv, pfin,
+    latv, knownv, statev, mwv, swv, sowv, cwv, cowv, acol, bias, tab, mixb, plainb, kvb, gb, gp, ab,
+    qs, cqs, acc, mx, acc2, mx2, att, gud, part, psend, precv, pfin,
     lsem, hs, hr, kss, krs, kvs, kvr, gas, gar, gbs, gbr, zs, zr, cs, cr, ps, pr,
 ):
     s = lax.axis_index("seq")
@@ -122,11 +116,47 @@
     for n, place in enumerate(("core", "over", "diag")):
         send(ab.at[q], ab.at[q], gas.at[n], gar.at[n], place)
 
+    lane = lax.broadcasted_iota(jnp.int32, (1, BLOCK), 1)
+    other = lax.rem(2 * s - at["core"] + NSEQ, NSEQ)
+    for n, name in enumerate((s, at["core"], at["up"], at["down"], other)):
+        for kb in range(2):
+            shut = []
+            for b in range(2):
+                hit = jnp.int32(0)
+                for m in range(6):
+                    hit = hit | jnp.where(lists[b, m] == 2 * name + kb, 1, 0)
+                shut.append(jnp.where(hit == 1, 0.0, -1e30))
+            for u, base in enumerate((HEAD_DIM, 0)):
+                line = jnp.where(lane == base, shut[0], jnp.where(lane == base + 1, shut[1], 0.0))
+                bias[u, 2 * n + kb : 2 * n + kb + 1, :] = line
+
+    step_row = lax.broadcasted_iota(jnp.int32, (8, BLOCK), 0)
+    moment = jnp.where(
+        step_row == 0, steps[0].astype(F32), jnp.where(step_row == 1, steps[1].astype(F32), steps[2].astype(F32))
+    )
+    which = lax.broadcasted_iota(jnp.int32, (8, BLOCK), 1).astype(F32)
+    phase = moment * jnp.exp(which * (-math.log(10000.0) / (FREQ // 2)))
+    for n, embed in enumerate((jnp.cos(phase), jnp.sin(phase))):
+        embed = (embed / (1.0 + jnp.exp(-embed))).astype(BF16).astype(F32)
+        for i in range(STEPS):
+            acol[i, BLOCK * n : BLOCK * (n + 1), :] = jnp.transpose(
+                jnp.broadcast_to(embed[i : i + 1, :], (BLOCK, BLOCK))
+            )
+    cosine = jnp.cos((moment / 1000.0 + 0.008) / 1.008 * (math.pi / 2.0))
+    level = cosine * cosine
+    root, rest = jnp.sqrt(level), jnp.sqrt(1.0 - level)
+    coefs = []
+    for i in range(STEPS):
+        ratio = root[i + 1 : i + 2] / root[i : i + 1]
+        line = (ratio, rest[i + 1 : i + 2] - ratio * rest[i : i + 1], root[i + 1 : i + 2], rest[i + 1 : i + 2])
+        coefs.append([jnp.concatenate([x] * 4, axis=1) for x in line])
+
     loads[5].wait()
 
     def modulate(k, sums):
         row = mwv[k].astype(F32)
-        return sums[0] + active[0, k] * row, sums[1] + active[1, k] * row
+        scale = [jnp.concatenate([acol[i, pl.ds(k, 1), :]] * 8, axis=1) for i in range(STEPS)]
+        return sums[0] + scale[0] * row, sums[1] + scale[1] * row
 
     zero = jnp.zeros((4, D), F32)
     tab[0], tab[1] = lax.fori_loop(0, FREQ, modulate, (zero, zero), unroll=4)
@@ -137,12 +167,12 @@
         lanes = pl.ds(pl.multiple_of(HALF * c, HALF), HALF)
         own = [ab[k, :, lanes].astype(F32) for k in range(4)]
         for i in range(STEPS):
-            gb[c, i, 0, 0:32, :] = jnp.concatenate(
+            gp[i, 0:32, :] = jnp.concatenate(
                 [o[GUIDE * i : GUIDE * (i + 1)] for o in own], axis=0
             ).astype(BF16)
             for d in range(1, 4):
                 send(
-                    gb.at[c, i, 0, 0:32], gb.at[c, i, 0, 32 * d : 32 * d + 32],
+                    gp.at[i, 0:32], gp.at[i, 32 * d : 32 * d + 32],
                     gbs.at[i, d - 1], gbr.at[i, d - 1], f"turn{d}",
                 )
 
@@ -156,9 +186,13 @@
     def guide_third(i):
         for d in range(1, 4):
             remote(
-                gb.at[c, i, 0, 0:32], gb.at[c, i, 0, 32 * d : 32 * d + 32],
+                gp.at[i, 0:32], gp.at[i, 32 * d : 32 * d + 32],
                 gbs.at[i, d - 1], gbr.at[i, d - 1], f"turn{d}",
             ).wait_recv()
+        for p in range(4):
+            cols = slice(BLOCK * p, BLOCK * (p + 1))
+            y = gp[i, :, cols].astype(F32)
+            gb[c, i, 0, :, cols] = jnp.where(c == 1, jnp.transpose(y), y).astype(BF16)
         ring(i, 0, 1)
         ring(i, 0, 2)
         across(i, 0)
@@ -176,7 +210,7 @@
     lane = lax.broadcasted_iota(jnp.int32, (1, BLOCK), 1)
     low = jnp.where(lane < HEAD_DIM, 1.0, 0.0).astype(BF16)
     low_f = lax.broadcasted_iota(jnp.int32, (TOK, BLOCK), 1) < HEAD_DIM
-    high = (1.0 - low.astype(F32)).astype(BF16)
+    keep = (low, (1.0 - low.astype(F32)).astype(BF16))
 
     def normalize(b, state):
         r = rows(b)
@@ -197,9 +231,13 @@
 
             def tile(t, _):
                 w = swv[1 + j, :, pl.ds(pl.multiple_of(256 * t, 256), 256)]
-                kvb[i, OWN, r, pl.ds(pl.multiple_of(HALF * j + 256 * t, 256), 256)] = jnp.dot(
-                    x, w, preferred_element_type=F32
-                ).astype(BF16)
+                y = jnp.dot(x, w, preferred_element_type=F32)
+                if j == 1:
+                    y = jnp.concatenate(
+                        [jnp.transpose(y[:, BLOCK * u : BLOCK * (u + 1)]) for u in range(2)], axis=1
+                    )
+                cols = pl.ds(pl.multiple_of(HALF * j + 256 * t, 256), 256)
+                kvb[i, OWN, r, cols] = y.astype(BF16)
                 return 0
 
             lax.fori_loop(0, 2, tile, 0)
@@ -243,66 +281,92 @@
 
         lax.fori_loop(0, 2, tile, 0)
 
-    def attend(q_ref, load, first, marks=None):
-        keep = (low, high)
-
+    ones = jnp.ones((16, TOK), BF16)
+
+    def attend(q_ref, tiles, first, sums, peaks):
         def pair(p, _):
-            k, v = load(pl.ds(pl.multiple_of(BLOCK * p, BLOCK), BLOCK))
+            lanes = pl.ds(pl.multiple_of(BLOCK * p, BLOCK), BLOCK)
+            loaded = [load(lanes) for load, _ in tiles]
             for u in range(2):
                 head = 2 * p + u
-                ku = k if marks is None else k * keep[u] + marks[u]
-                vu = v * keep[u] + keep[1 - u]
-                scores = lax.dot_general(
-                    q_ref[head], ku, (((1,), (1,)), ((), ())), preferred_element_type=F32
+                scores = []
+                for (k, _), (_, marks) in zip(loaded, tiles):
+                    k = k if marks is None else k * keep[u] + marks[u]
+                    scores.append(
+                        lax.dot_general(
+                            k, q_ref[head], (((1,), (1,)), ((), ())), preferred_element_type=F32
+                        )
+                    )
+                peak = functools.reduce(
+                    jnp.maximum, [jnp.max(x, axis=0, keepdims=True) for x in scores]
                 )
-                peak = jnp.max(scores, axis=1, keepdims=True)
                 if not first:
-                    old = mx[head]
-                    peak = jnp.maximum(peak, old[:, 0:1])
-                weights = jnp.exp(scores - peak).astype(BF16)
-                mixed = jnp.dot(weights, vu, preferred_element_type=F32)
-                wide = jnp.broadcast_to(peak, (TOK, BLOCK))
+                    old = peaks[head, 0:1, :]
+                    peak = jnp.maximum(peak, old)
+                mixed = None
+                for x, (_, v) in zip(scores, loaded):
+                    v = jnp.concatenate([v[HEAD_DIM * u : HEAD_DIM * (u + 1)], ones], axis=0)
+                    y = jnp.dot(v, jnp.exp(x - peak).astype(BF16), preferred_element_type=F32)
+                    mixed = y if mixed is None else mixed + y
                 if not first:
-                    mixed = mixed + acc[head] * jnp.exp(old - wide)
-                acc[head] = mixed
-                mx[head] = wide
+                    mixed = mixed + sums[head] * jnp.exp(old - peak)
+                sums[head] = mixed
+                peaks[head, 0:1, :] = peak
             return 0
 
         lax.fori_loop(0, 4, pair, 0)
 
-    def attend_tile(i, slot):
-        marks = [
-            jnp.concatenate(
-                [jnp.broadcast_to(bias[u, 2 * slot + b : 2 * slot + b + 1, :], (BLOCK, BLOCK)) for b in range(2)],
-                axis=0,
-            ).astype(BF16)
-            for u in range(2)
-        ]
-
-        def load(lanes):
-            return kvb[i, slot, :, lanes], kvb[i, slot, :, pl.ds(HALF + lanes.start, BLOCK)]
-
-        attend(qs, load, slot == OWN, marks)
-
-    def attend_guide(i, n):
-        def load(lanes):
-            return [
-                gb[j, i, 2 * n : 2 * n + 2, :, lanes].reshape(TOK, BLOCK) for j in range(2)
+    def attend_tiles(i, *slots):
+        def tile(slot):
+            marks = [
+                jnp.concatenate(
+                    [
+                        jnp.broadcast_to(
+                            bias[u, 2 * slot + b : 2 * slot + b + 1, :], (BLOCK, BLOCK)
+                        )
+                        for b in range(2)
+                    ],
+                    axis=0,
+                ).astype(BF16)
+                for u in range(2)
             ]
 
-        attend(cqs, load, n == 0)
+            def load(lanes):
+                high_lanes = pl.ds(HALF + lanes.start, BLOCK)
+                v = [kvb[i, slot, BLOCK * b : BLOCK * (b + 1), high_lanes] for b in range(2)]
+                return kvb[i, slot, :, lanes], jnp.concatenate(v, axis=1)
+
+            return load, marks
+
+        attend(qs, [tile(slot) for slot in slots], slots[0] == OWN, acc, mx)
+
+    def attend_guide(i, *chunks):
+        def tile(n):
+            def load(lanes):
+                k = gb[0, i, 2 * n : 2 * n + 2, :, lanes].reshape(TOK, BLOCK)
+                v = [gb[1, i, 2 * n + b, :, lanes] for b in range(2)]
+                return k, jnp.concatenate(v, axis=1)
+
+            return load, None
+
+        attend(cqs, [tile(n) for n in chunks], chunks[0] == 0, acc2, mx2)
 
     def crossed(i, *slots):
         for slot in slots:
             remote(gb.at[c, i, 0], gb.at[1 - c, i, slot], cs.at[i, slot], cr.at[i, slot],
                    "core").wait_recv()
 
-    def finish(dst):
+    def finish(dst, sums):
         def pair(p, _):
-            a, b = acc[2 * p], acc[2 * p + 1]
-            a = a / pltpu.roll(a, HEAD_DIM, 1)
-            b = b / pltpu.roll(b, HEAD_DIM, 1)
-            dst[:, pl.ds(pl.multiple_of(BLOCK * p, BLOCK), BLOCK)] = jnp.where(low_f, a, b).astype(BF16)
+            y = [
+                sums[2 * p + u, 0:HEAD_DIM, :] / sums[2 * p + u, HEAD_DIM : HEAD_DIM + 1, :]
+                for u in range(2)
+            ]
+            y = jnp.concatenate(y, axis=0)
+            for b in range(2):
+                dst[rows(b), pl.ds(pl.multiple_of(BLOCK * p, BLOCK), BLOCK)] = jnp.transpose(
+                    y[:, BLOCK * b : BLOCK * (b + 1)]
+                ).astype(BF16)
             return 0
 
         lax.fori_loop(0, 4, pair, 0)
@@ -323,14 +387,14 @@
         lax.fori_loop(0, 4, tile, 0)
 
     def seam(b):
-        flags = jnp.broadcast_to(mask[b : b + 1, :], (BLOCK, BLOCK))
+        flags = jnp.broadcast_to(mask[b : b + 1, :].astype(F32), (BLOCK, BLOCK))
         wide = jnp.transpose(flags)
         return jnp.concatenate([wide] * 4, axis=1) > 0.5
 
     def updated(i, b, n, state, noise):
         r = rows(b)
-        moved = coef[4 * i] * state + coef[4 * i + 1] * noise
-        kept = coef[4 * i + 2] * knownv[n, r].astype(F32) + coef[4 * i + 3] * latv[n, r].astype(F32)
+        moved = coefs[i][0] * state + coefs[i][1] * noise
+        kept = coefs[i][2] * knownv[n, r].astype(F32) + coefs[i][3] * latv[n, r].astype(F32)
         return jnp.where(seam(b), moved, kept).astype(BF16)
 
     loads[2].wait()
@@ -346,39 +410,40 @@
     loads[7].wait()
     send(known, knownv.at[h], kss.at[0], krs.at[0], "head")
     queries(mixb, swv, qs, True)
-    queries(plainb, cwv, cqs, False)
     guide_third(0)
-    guide_third(1)
-    attend_tile(0, OWN)
+    attend_tiles(0, OWN)
     hop(0, 1, 2)
     relay(0, 0)
+    queries(plainb, cwv, cqs, False)
     arrived(0, CORE, 0)
     arrived(0, CORE, 1)
-    attend_tile(0, CORE)
-    hop(1, 1, 2)
+    attend_tiles(0, CORE)
     hop(0, 3, 4)
     relay(0, 1)
-    attend_tile(0, UP)
+    attend_tiles(0, UP, DOWN)
     hop(0, 5, 6)
-    hop(1, 3, 4)
-    attend_tile(0, DOWN)
+    crossed(0, 0, 1)
+    attend_guide(0, 0)
     hop(0, 7)
-    hop(1, 5, 6)
+    guide_third(1)
     arrived(0, OVER, 0)
     arrived(0, OVER, 1)
-    attend_tile(0, OVER)
-    hop(1, 7)
-    finish(att)
-    for n in range(4):
-        crossed(0, 2 * n, 2 * n + 1)
-        attend_guide(0, n)
-    finish(gud)
+    attend_tiles(0, OVER)
+    finish(att, acc)
     loads[8].wait()
     loads[9].wait()
     for b in range(2):
         project(0, b, att, sowv, 2, True)
+    crossed(0, 2, 3)
+    attend_guide(0, 1)
+    hop(1, 1, 2)
+    crossed(0, 4, 5, 6, 7)
+    attend_guide(0, 2, 3)
+    finish(gud, acc2)
+    for b in range(2):
         project(0, b, gud, cowv, 3, False)
         send(psend.at[0, rows(b)], precv.at[rows(b)], ps.at[0, b], pr.at[0, b], "head")
+    hop(1, 3, 4)
 
     loads[10].wait()
     remote(known, knownv.at[1 - h], kss.at[0], krs.at[0], "head").wait_recv()
@@ -391,28 +456,28 @@
             statev[n, r] = updated(0, b, n, latv[n, r].astype(F32), noise)
         mix(1, b, statev)
         keys_values(1, b)
+        if b == 0:
+            hop(1, 5, 6)
+    hop(1, 7)
+    queries(mixb, swv, qs, True)
+    attend_tiles(1, OWN)
     queries(plainb, cwv, cqs, False)
-    queries(mixb, swv, qs, True)
+    relay(1, 0)
     crossed(1, *range(8))
-    attend_guide(1, 0)
-    attend_guide(1, 1)
-    relay(1, 0)
-    attend_guide(1, 2)
-    attend_guide(1, 3)
+    attend_guide(1, 0, 1)
     relay(1, 1)
-    finish(gud)
-    for b in range(2):
-        project(1, b, gud, cowv, 3, True)
-    attend_tile(1, OWN)
+    attend_guide(1, 2, 3)
     arrived(1, CORE, 0)
     arrived(1, CORE, 1)
-    attend_tile(1, CORE)
-    attend_tile(1, UP)
-    attend_tile(1, DOWN)
+    attend_tiles(1, CORE)
+    finish(gud, acc2)
+    for b in range(2):
+        project(1, b, gud, cowv, 3, True)
+    attend_tiles(1, UP, DOWN)
     arrived(1, OVER, 0)
     arrived(1, OVER, 1)
-    attend_tile(1, OVER)
-    finish(att)
+    attend_tiles(1, OVER)
+    finish(att, acc)
     mine = pl.ds(pl.multiple_of(HALF * h, HALF), HALF)
     theirs = pl.ds(pl.multiple_of(HALF * (1 - h), HALF), HALF)
     for b in range(2):
@@ -432,30 +497,7 @@
     latents, known, seam_mask, timesteps, block_lists, guidance,
     modulation_weight, self_weight, self_out_weight, cross_weight, cross_out_weight,
 ):
-    s = lax.axis_index("seq")
-    at = places(s)
-    other = 2 * s - at["core"]
-    names = jnp.stack([s, at["core"], at["up"], at["down"], lax.rem(other + NSEQ, NSEQ)])
-    names = (2 * names[:, None] + jnp.arange(2)).reshape(-1)
-    listed = jnp.any(block_lists[:, :, None] == names, axis=1)
-    shut = jnp.where(listed, 0.0, -1e30).astype(F32)
-    lanes = jnp.arange(BLOCK)
-    bias = jnp.stack(
-        [
-            sum(jnp.where(lanes == base + b, shut[b][:, None], 0.0) for b in range(2))
-            for base in (HEAD_DIM, 0)
-        ]
-    )
-    half = FREQ // 2
-    frequency = jnp.exp(-math.log(10000.0) * jnp.arange(half, dtype=F32) / half)
-    phase = timesteps[:STEPS].astype(F32)[:, None] * frequency
-    embed = jnp.concatenate([jnp.cos(phase), jnp.sin(phase)], axis=1)
-    active = jax.nn.silu(embed).astype(BF16).astype(F32)
-    level = signal_level(timesteps)
-    root, rest = jnp.sqrt(level), jnp.sqrt(1.0 - level)
-    ratio = root[1:] / root[:-1]
-    coef = jnp.stack([ratio, rest[1:] - ratio * rest[:-1], root[1:], rest[1:]], axis=1)
-    mask = seam_mask.astype(F32).reshape(2, BLOCK)
+    mask = seam_mask.reshape(2, BLOCK)
     vmem = pl.BlockSpec(memory_space=pltpu.VMEM)
     smem = pl.BlockSpec(memory_space=pltpu.SMEM)
     hbm = pl.BlockSpec(memory_space=pl.ANY)
@@ -463,7 +505,7 @@
     return pl.pallas_call(
         kernel,
         out_shape=jax.ShapeDtypeStruct((TOK, HALF), BF16),
-        in_specs=[smem, smem, vmem, vmem, vmem] + [hbm] * 7,
+        in_specs=[smem, smem, vmem, vmem] + [hbm] * 7,
         out_specs=vmem,
         scratch_shapes=[
             pltpu.VMEM((2, TOK, HALF), BF16),
@@ -474,16 +516,21 @@
             pltpu.VMEM((HALF, D), BF16),
             pltpu.VMEM((3, D, HALF), BF16),
             pltpu.VMEM((HALF, D), BF16),
+            pltpu.VMEM((STEPS, FREQ, BLOCK), F32),
+            pltpu.VMEM((2, 16, BLOCK), F32),
             pltpu.VMEM((STEPS, 4, D), F32),
             pltpu.VMEM((TOK, D), BF16),
             pltpu.VMEM((TOK, D), BF16),
             pltpu.VMEM((STEPS, 5, TOK, D), BF16),
             pltpu.VMEM((2, STEPS, 8, BLOCK, HALF), BF16),
+            pltpu.VMEM((STEPS, BLOCK, HALF), BF16),
             pltpu.VMEM((4, STEPS * GUIDE, D), BF16),
             pltpu.VMEM((8, TOK, BLOCK), BF16),
             pltpu.VMEM((8, TOK, BLOCK), BF16),
-            pltpu.VMEM((8, TOK, BLOCK), F32),
-            pltpu.VMEM((8, TOK, BLOCK), F32),
+            pltpu.VMEM((8, HEAD_DIM + 16, TOK), F32),
+            pltpu.VMEM((8, 8, TOK), F32),
+            pltpu.VMEM((8, HEAD_DIM + 16, TOK), F32),
+            pltpu.VMEM((8, 8, TOK), F32),
             pltpu.VMEM((TOK, HALF), BF16),
             pltpu.VMEM((TOK, HALF), BF16),
             pltpu.VMEM((TOK, D), F32),
@@ -501,7 +548,7 @@
         ),
         name="denoise",
     )(
-        active, coef.reshape(-1), mask, bias, guidance.reshape(STEPS * GUIDE, D),
+        timesteps, block_lists, mask, guidance.reshape(STEPS * GUIDE, D),
         latents, known, modulation_weight, jnp.transpose(self_weight, (1, 0, 2)),
         self_out_weight, jnp.transpose(cross_weight, (1, 0, 2)), cross_out_weight,
     )

time: 144 us -> 114 us (0.79)
  Pallas kernels: 135 us -> 110 us
  other arithmetic: 4.96 us -> 0 us
    pallas_call x1, Pallas kernels: 135 us -> 110 us  [on_device(): pl.pallas_call(kernel, out_shape=jax.ShapeDtypeStruct((TOK, HALF), BF16),...]
where the time goes in v3:
time: 114 us; the launch traced here: 112 us
  Pallas kernels  110 us (96%)
  local copies, waits for them, and re-layouts  1.67 us (1%)
    pallas_call x1, Pallas kernels, on_device(): pl.pallas_call(kernel, out_shape=jax.ShapeDtypeStruct((TOK, HALF), BF16),...  110 us

profile of v3, /device:TPU:32, one launch (start us, length us, event | category | flops | bytes accessed | tf_op | source)
XLA Modules:
  0.0 111.9 jit_solution(11441670598868107021)
XLA Ops:
  0.0 110.2 %denoise.1 = bf16[256,512]{1,0:T(8,128)(2,1)} custom-call(s32[3]{0:T(128)} %steps.1, s32[2,6]{1,0:T(2,128)} %lists.1, s32[2,128]{1,0:T(2,128)} %bitcast.7, bf16[16,1024]{1,0:T(8,128)(2,1)} %bitcast.6, bf16[256,512]{1,0:T(8,128)(2,1)} %lat.1, bf16[256,512]{1,0:T(8,128)(2,1)} %known.1, bf16[256,4,1024]{2,1,0:T(4,128)(2,1)} %mw.1, ...), custom_call_target="tpu_custom_call" | custom-call | tf_op jit(solution)/shard_map/denoise/pallas_call | solution.py:505
  110.2 1.7 %copy.13 = bf16[256,512]{1,0:T(8,128)(2,1)} copy(bf16[256,512]{1,0:T(8,128)(2,1)} %denoise.1) | data formatting | bytes 524288

commit v4 on v3

--- a/solution.py
+++ b/solution.py
@@ -240,7 +240,7 @@
                 kvb[i, OWN, r, cols] = y.astype(BF16)
                 return 0
 
-            lax.fori_loop(0, 2, tile, 0)
+            lax.fori_loop(0, 2, tile, 0, unroll=True)
         for n, (slot, place) in enumerate(((CORE, "core"), (DOWN, "up"), (UP, "down"))):
             send(kvb.at[i, OWN, r], kvb.at[i, slot, r], kvs.at[i, n, b], kvr.at[i, slot, b], place)
 
@@ -279,7 +279,7 @@
                 dst[4 * t + 2 * u + 1] = jnp.where(low_f, mark_b, z).astype(BF16)
             return 0
 
-        lax.fori_loop(0, 2, tile, 0)
+        lax.fori_loop(0, 2, tile, 0, unroll=True)
 
     ones = jnp.ones((16, TOK), BF16)
 
@@ -314,7 +314,7 @@
                 peaks[head, 0:1, :] = peak
             return 0
 
-        lax.fori_loop(0, 4, pair, 0)
+        lax.fori_loop(0, 4, pair, 0, unroll=True)
 
     def attend_tiles(i, *slots):
         def tile(slot):
@@ -369,7 +369,7 @@
                 ).astype(BF16)
             return 0
 
-        lax.fori_loop(0, 4, pair, 0)
+        lax.fori_loop(0, 4, pair, 0, unroll=True)
 
     def project(i, b, x_ref, w_ref, gate, first):
         r = rows(b)
@@ -384,7 +384,7 @@
                 psend[i, r, cols] = y.astype(BF16)
             return 0
 
-        lax.fori_loop(0, 4, tile, 0)
+        lax.fori_loop(0, 4, tile, 0, unroll=True)
 
     def seam(b):
         flags = jnp.broadcast_to(mask[b : b + 1, :].astype(F32), (BLOCK, BLOCK))

time: 114 us -> 103 us (0.904); the launches traced: 112 us -> 103 us
  Pallas kernels: 110 us -> 101 us
    pallas_call x1, Pallas kernels: 110 us -> 101 us  [on_device(): pl.pallas_call(kernel, out_shape=jax.ShapeDtypeStruct((TOK, HALF), BF16),...]
where the time goes in v4:
time: 103 us
  Pallas kernels  101 us (98%)
  local copies, waits for them, and re-layouts  1.67 us (2%)
    pallas_call x1, Pallas kernels, on_device(): pl.pallas_call(kernel, out_shape=jax.ShapeDtypeStruct((TOK, HALF), BF16),...  101 us

profile of v4, /device:TPU:32, one launch (start us, length us, event | category | flops | bytes accessed | tf_op | source)
XLA Modules:
  0.0 102.8 jit_solution(143064448384191429)
XLA Ops:
  0.0 101.2 %denoise.1 = bf16[256,512]{1,0:T(8,128)(2,1)} custom-call(s32[3]{0:T(128)} %steps.1, s32[2,6]{1,0:T(2,128)} %lists.1, s32[2,128]{1,0:T(2,128)} %bitcast.7, bf16[16,1024]{1,0:T(8,128)(2,1)} %bitcast.6, bf16[256,512]{1,0:T(8,128)(2,1)} %lat.1, bf16[256,512]{1,0:T(8,128)(2,1)} %known.1, bf16[256,4,1024]{2,1,0:T(4,128)(2,1)} %mw.1, ...), custom_call_target="tpu_custom_call" | custom-call | tf_op jit(solution)/shard_map/denoise/pallas_call | solution.py:505
  101.2 1.7 %copy.13 = bf16[256,512]{1,0:T(8,128)(2,1)} copy(bf16[256,512]{1,0:T(8,128)(2,1)} %denoise.1) | data formatting | bytes 524288

commit v5 on v4

--- a/solution.py
+++ b/solution.py
@@ -13,6 +13,7 @@
 HEAD_DIM = 64
 FREQ = 256
 BLOCK = 128
+MAXK = 6
 TOK = 256
 STEPS = 2
 NSEQ = 128
@@ -53,7 +54,7 @@
 def kernel(
     steps, lists, mask, guid, lat, known, mw, sw, sow, cw, cow,
     out,
-    latv, knownv, statev, mwv, swv, sowv, cwv, cowv, acol, bias, tab, mixb, plainb, kvb, gb, gp, ab,
+    latv, knownv, statev, mwv, swv, sowv, cwv, cowv, acol, bias, tile_bias, seam, tab, mixb, plainb, kv0, kv1, gb, gp, ab,
     qs, cqs, acc, mx, acc2, mx2, att, gud, part, psend, precv, pfin,
     lsem, hs, hr, kss, krs, kvs, kvr, gas, gar, gbs, gbr, zs, zr, cs, cr, ps, pr,
 ):
@@ -61,6 +62,7 @@
     h = lax.axis_index("head")
     q = lax.rem(s, 4)
     c = lax.rem(s, 2)
+    kv = (kv0, kv1)
     at = places(s)
     to = {k: {"seq": v, "head": h} for k, v in at.items()}
     to["head"] = {"seq": s, "head": 1 - h}
@@ -118,17 +120,38 @@
 
     lane = lax.broadcasted_iota(jnp.int32, (1, BLOCK), 1)
     other = lax.rem(2 * s - at["core"] + NSEQ, NSEQ)
-    for n, name in enumerate((s, at["core"], at["up"], at["down"], other)):
+    names = (s, at["core"], at["up"], at["down"], other)
+    picks = []
+    for b in range(2):
+        picks.append([])
+        for m in range(MAXK):
+            entry = lists[b, m]
+            spot = jnp.int32(0)
+            for n, name in enumerate(names):
+                for kb in range(2):
+                    spot = jnp.where(entry == 2 * name + kb, 2 * n + kb, spot)
+            picks[b].append(spot)
+            shut = jnp.where(entry >= 0, 0.0, -1e30)
+            for u, base in enumerate((HEAD_DIM, 0)):
+                bias[u, MAXK * b + m : MAXK * b + m + 1, :] = jnp.where(lane == base + b, shut, 0.0)
+
+    for b in range(2):
+        flags = mask[pl.ds(BLOCK * b, BLOCK)].astype(F32)
+        seam[pl.ds(BLOCK * b, BLOCK), :] = jnp.transpose(
+            jnp.broadcast_to(flags[None, :], (BLOCK, BLOCK))
+        )
+
+    for n, name in enumerate(names):
         for kb in range(2):
             shut = []
             for b in range(2):
                 hit = jnp.int32(0)
-                for m in range(6):
+                for m in range(MAXK):
                     hit = hit | jnp.where(lists[b, m] == 2 * name + kb, 1, 0)
                 shut.append(jnp.where(hit == 1, 0.0, -1e30))
             for u, base in enumerate((HEAD_DIM, 0)):
                 line = jnp.where(lane == base, shut[0], jnp.where(lane == base + 1, shut[1], 0.0))
-                bias[u, 2 * n + kb : 2 * n + kb + 1, :] = line
+                tile_bias[u, 2 * n + kb : 2 * n + kb + 1, :] = line
 
     step_row = lax.broadcasted_iota(jnp.int32, (8, BLOCK), 0)
     moment = jnp.where(
@@ -224,9 +247,16 @@
             mixb[r, cols] = (normed[n] * (1.0 + tab[i, 1:2, cols]) + tab[i, 0:1, cols]).astype(BF16)
             plainb[r, cols] = normed[n].astype(BF16)
 
+    def chunk(i, n, j):
+        return kv[i].at[n, :, pl.ds(HALF * j, HALF)]
+
+    def over(i, b, j, n):
+        return remote(
+            chunk(i, n, j), chunk(i, 2 * OVER + b, j), kvs.at[i, 3, b, j], kvr.at[i, OVER, b, j], "over"
+        )
+
     def keys_values(i, b):
-        r = rows(b)
-        x = mixb[r, :]
+        x = mixb[rows(b), :]
         for j in range(2):
 
             def tile(t, _):
@@ -237,31 +267,39 @@
                         [jnp.transpose(y[:, BLOCK * u : BLOCK * (u + 1)]) for u in range(2)], axis=1
                     )
                 cols = pl.ds(pl.multiple_of(HALF * j + 256 * t, 256), 256)
-                kvb[i, OWN, r, cols] = y.astype(BF16)
+                kv[i][b, :, cols] = y.astype(BF16)
                 return 0
 
             lax.fori_loop(0, 2, tile, 0, unroll=True)
-        for n, (slot, place) in enumerate(((CORE, "core"), (DOWN, "up"), (UP, "down"))):
-            send(kvb.at[i, OWN, r], kvb.at[i, slot, r], kvs.at[i, n, b], kvr.at[i, slot, b], place)
-
-        @pl.when(q * (3 - q) > 0)
-        def _():
-            remote(kvb.at[i, OWN, r], kvb.at[i, OVER, r], kvs.at[i, 3, b], kvr.at[i, OVER, b], "over").start()
-
-        sent.append(remote(kvb.at[i, OWN, r], kvb.at[i, OVER, r], kvs.at[i, 3, b], kvr.at[i, OVER, b], "over"))
+            for n, (slot, place) in enumerate(((DOWN, "up"), (UP, "down"), (CORE, "core"))):
+                send(
+                    chunk(i, b, j), chunk(i, 2 * slot + b, j),
+                    kvs.at[i, n, b, j], kvr.at[i, slot, b, j], place,
+                )
+
+            @pl.when(q * (3 - q) > 0)
+            def _():
+                over(i, b, j, b).start()
+
+            sent.append(over(i, b, j, b))
 
     def arrived(i, slot, b):
-        remote(kvb.at[i, OWN, rows(b)], kvb.at[i, slot, rows(b)], kvs.at[i, 0, b],
-               kvr.at[i, slot, b], "core").wait_recv()
+        for j in range(2):
+            arrived_part(i, slot, b, j)
+
+    def arrived_part(i, slot, b, j):
+        remote(
+            chunk(i, b, j), chunk(i, 2 * slot + b, j), kvs.at[i, 0, b, j], kvr.at[i, slot, b, j], "core"
+        ).wait_recv()
 
     def relay(i, b):
-        arrived(i, UP, b)
-        arrived(i, DOWN, b)
-        r = rows(b)
-
-        @pl.when(q * (3 - q) == 0)
-        def _():
-            remote(kvb.at[i, UP + q // 3, r], kvb.at[i, OVER, r], kvs.at[i, 3, b], kvr.at[i, OVER, b], "over").start()
+        for j in range(2):
+            arrived_part(i, UP, b, j)
+            arrived_part(i, DOWN, b, j)
+
+            @pl.when(q * (3 - q) == 0)
+            def _():
+                over(i, b, j, 2 * (UP + q // 3) + b).start()
 
     row_id = lax.broadcasted_iota(jnp.int32, (TOK, BLOCK), 0) // BLOCK
     lane_id = lax.broadcasted_iota(jnp.int32, (TOK, BLOCK), 1)
@@ -320,12 +358,7 @@
         def tile(slot):
             marks = [
                 jnp.concatenate(
-                    [
-                        jnp.broadcast_to(
-                            bias[u, 2 * slot + b : 2 * slot + b + 1, :], (BLOCK, BLOCK)
-                        )
-                        for b in range(2)
-                    ],
+                    [jnp.broadcast_to(tile_bias[u, n : n + 1, :], (BLOCK, BLOCK)) for n in (2 * slot, 2 * slot + 1)],
                     axis=0,
                 ).astype(BF16)
                 for u in range(2)
@@ -333,12 +366,47 @@
 
             def load(lanes):
                 high_lanes = pl.ds(HALF + lanes.start, BLOCK)
-                v = [kvb[i, slot, BLOCK * b : BLOCK * (b + 1), high_lanes] for b in range(2)]
-                return kvb[i, slot, :, lanes], jnp.concatenate(v, axis=1)
+                v = [kv[i][2 * slot + b, :, high_lanes] for b in range(2)]
+                k = kv[i][2 * slot : 2 * slot + 2, :, lanes].reshape(TOK, BLOCK)
+                return k, jnp.concatenate(v, axis=1)
 
             return load, marks
 
         attend(qs, [tile(slot) for slot in slots], slots[0] == OWN, acc, mx)
+
+    wide_ones = jnp.ones((16, MAXK * BLOCK), BF16)
+
+    def attend_listed(i, b):
+        marks = [
+            jnp.concatenate(
+                [
+                    jnp.broadcast_to(bias[u, n : n + 1, :], (BLOCK, BLOCK))
+                    for n in range(MAXK * b, MAXK * b + MAXK)
+                ],
+                axis=0,
+            ).astype(BF16)
+            for u in range(2)
+        ]
+
+        def pair(p, _):
+            lanes = pl.ds(pl.multiple_of(BLOCK * p, BLOCK), BLOCK)
+            high_lanes = pl.ds(pl.multiple_of(HALF + BLOCK * p, BLOCK), BLOCK)
+            k = jnp.concatenate([kv[i][spot, :, lanes] for spot in picks[b]], axis=0)
+            v = jnp.concatenate([kv[i][spot, :, high_lanes] for spot in picks[b]], axis=1)
+            mixed = []
+            for u in range(2):
+                scores = lax.dot_general(
+                    k * keep[u] + marks[u], qs[2 * p + u, rows(b), :],
+                    (((1,), (1,)), ((), ())), preferred_element_type=F32,
+                )
+                weights = jnp.exp(scores - jnp.max(scores, axis=0, keepdims=True)).astype(BF16)
+                vu = jnp.concatenate([v[HEAD_DIM * u : HEAD_DIM * (u + 1)], wide_ones], axis=0)
+                y = jnp.dot(vu, weights, preferred_element_type=F32)
+                mixed.append(y[0:HEAD_DIM] / y[HEAD_DIM : HEAD_DIM + 1])
+            att[rows(b), lanes] = jnp.transpose(jnp.concatenate(mixed, axis=0)).astype(BF16)
+            return 0
+
+        lax.fori_loop(0, 4, pair, 0, unroll=True)
 
     def attend_guide(i, *chunks):
         def tile(n):
@@ -386,16 +454,12 @@
 
         lax.fori_loop(0, 4, tile, 0, unroll=True)
 
-    def seam(b):
-        flags = jnp.broadcast_to(mask[b : b + 1, :].astype(F32), (BLOCK, BLOCK))
-        wide = jnp.transpose(flags)
-        return jnp.concatenate([wide] * 4, axis=1) > 0.5
-
     def updated(i, b, n, state, noise):
         r = rows(b)
         moved = coefs[i][0] * state + coefs[i][1] * noise
         kept = coefs[i][2] * knownv[n, r].astype(F32) + coefs[i][3] * latv[n, r].astype(F32)
-        return jnp.where(seam(b), moved, kept).astype(BF16)
+        flags = jnp.concatenate([seam[r, :]] * 4, axis=1) > 0.5
+        return jnp.where(flags, moved, kept).astype(BF16)
 
     loads[2].wait()
     loads[3].wait()
@@ -459,28 +523,23 @@
         if b == 0:
             hop(1, 5, 6)
     hop(1, 7)
+    queries(plainb, cwv, cqs, False)
     queries(mixb, swv, qs, True)
-    attend_tiles(1, OWN)
-    queries(plainb, cwv, cqs, False)
-    relay(1, 0)
     crossed(1, *range(8))
     attend_guide(1, 0, 1)
+    relay(1, 0)
+    attend_guide(1, 2, 3)
+    finish(gud, acc2)
+    for b in range(2):
+        project(1, b, gud, cowv, 3, True)
     relay(1, 1)
-    attend_guide(1, 2, 3)
-    arrived(1, CORE, 0)
-    arrived(1, CORE, 1)
-    attend_tiles(1, CORE)
-    finish(gud, acc2)
-    for b in range(2):
-        project(1, b, gud, cowv, 3, True)
-    attend_tiles(1, UP, DOWN)
-    arrived(1, OVER, 0)
-    arrived(1, OVER, 1)
-    attend_tiles(1, OVER)
-    finish(att, acc)
     mine = pl.ds(pl.multiple_of(HALF * h, HALF), HALF)
     theirs = pl.ds(pl.multiple_of(HALF * (1 - h), HALF), HALF)
-    for b in range(2):
+    for slot in (CORE, OVER):
+        for b in range(2):
+            arrived(1, slot, b)
+    for b in range(2):
+        attend_listed(1, b)
         project(1, b, att, sowv, 2, False)
         send(psend.at[1, rows(b), theirs], pfin.at[rows(b)], ps.at[1, b], pr.at[1, b], "head")
     for b in range(2):
@@ -497,7 +556,6 @@
     latents, known, seam_mask, timesteps, block_lists, guidance,
     modulation_weight, self_weight, self_out_weight, cross_weight, cross_out_weight,
 ):
-    mask = seam_mask.reshape(2, BLOCK)
     vmem = pl.BlockSpec(memory_space=pltpu.VMEM)
     smem = pl.BlockSpec(memory_space=pltpu.SMEM)
     hbm = pl.BlockSpec(memory_space=pl.ANY)
@@ -518,10 +576,13 @@
             pltpu.VMEM((HALF, D), BF16),
             pltpu.VMEM((STEPS, FREQ, BLOCK), F32),
             pltpu.VMEM((2, 16, BLOCK), F32),
+            pltpu.VMEM((2, 16, BLOCK), F32),
+            pltpu.VMEM((TOK, BLOCK), F32),
             pltpu.VMEM((STEPS, 4, D), F32),
             pltpu.VMEM((TOK, D), BF16),
             pltpu.VMEM((TOK, D), BF16),
-            pltpu.VMEM((STEPS, 5, TOK, D), BF16),
+            pltpu.VMEM((10, BLOCK, D), BF16),
+            pltpu.VMEM((10, BLOCK, D), BF16),
             pltpu.VMEM((2, STEPS, 8, BLOCK, HALF), BF16),
             pltpu.VMEM((STEPS, BLOCK, HALF), BF16),
             pltpu.VMEM((4, STEPS * GUIDE, D), BF16),
@@ -538,7 +599,7 @@
             pltpu.VMEM((TOK, D), BF16),
             pltpu.VMEM((TOK, HALF), BF16),
             dma(11), dma(2), dma(2), dma(1), dma(1),
-            dma(STEPS, 4, 2), dma(STEPS, 5, 2),
+            dma(STEPS, 4, 2, 2), dma(STEPS, 5, 2, 2),
             dma(3), dma(3), dma(STEPS, 3), dma(STEPS, 3),
             dma(STEPS, 8), dma(STEPS, 8), dma(STEPS, 8), dma(STEPS, 8),
             dma(STEPS, 2), dma(STEPS, 2),
@@ -548,7 +609,7 @@
         ),
         name="denoise",
     )(
-        timesteps, block_lists, mask, guidance.reshape(STEPS * GUIDE, D),
+        timesteps, block_lists, seam_mask, guidance.reshape(STEPS * GUIDE, D),
         latents, known, modulation_weight, jnp.transpose(self_weight, (1, 0, 2)),
         self_out_weight, jnp.transpose(cross_weight, (1, 0, 2)), cross_out_weight,
     )

time: 103 us -> 102 us (level)
    pallas_call x1, Pallas kernels: 101 us -> 100 us  [on_device(): pl.pallas_call(kernel, out_shape=jax.ShapeDtypeStruct((TOK, HALF), BF16),...]
where the time goes in v5:
time: 102 us
  Pallas kernels  100 us (98%)
  local copies, waits for them, and re-layouts  1.67 us (2%)
    pallas_call x1, Pallas kernels, on_device(): pl.pallas_call(kernel, out_shape=jax.ShapeDtypeStruct((TOK, HALF), BF16),...  100 us

profile of v5, /device:TPU:32, one launch (start us, length us, event | category | flops | bytes accessed | tf_op | source)
XLA Modules:
  0.0 101.8 jit_solution(15386977405456955457)
XLA Ops:
  0.0 100.1 %denoise.1 = bf16[256,512]{1,0:T(8,128)(2,1)} custom-call(s32[3]{0:T(128)} %steps.1, s32[2,6]{1,0:T(2,128)} %lists.1, s32[256]{0:T(256)} %mask.1, bf16[16,1024]{1,0:T(8,128)(2,1)} %bitcast.5, bf16[256,512]{1,0:T(8,128)(2,1)} %lat.1, bf16[256,512]{1,0:T(8,128)(2,1)} %known.1, bf16[256,4,1024]{2,1,0:T(4,128)(2,1)} %mw.1, bf16[3,1024,512]{2,1,0:T(8,128)(2,1)} %bitcast.3, ...), custom_call_target="tpu_custom_call" | custom-call | tf_op jit(solution)/shard_map/denoise/pallas_call | solution.py:563
  100.1 1.7 %copy.13 = bf16[256,512]{1,0:T(8,128)(2,1)} copy(bf16[256,512]{1,0:T(8,128)(2,1)} %denoise.1) | data formatting | bytes 524288
